TPU v7x, 32 devices: a whole 2x2x4 slice. The times are simulated.
32 devices in a mesh: groups: 2 (over y), tensor: 4 (over z), dp: 4 (over x, core).
Axes of the slice: x: 2, y: 2, z: 4, core: 2. Of those that a mesh axis runs over, the one named last changes fastest.
Arguments:
- root_features: bfloat16 [32, 16384], P('groups', 'dp'), parts along dimension 0, may hold values from -6 to 6
- branch_embeds: bfloat16 [32, 4, 8, 16384], P('groups', None, None, 'dp'), parts along dimension 0, may hold values from -6 to 6
- parents: int32 [32, 3, 8], P('groups'), parts along dimension 0, may hold values from 0 to 7
- cache_lengths: int32 [32], P(('groups', 'dp')), parts along dimension 0, may hold values from 128 to 512, as said below
- cache_kv: bfloat16 [32, 2, 512, 512], P(('groups', 'dp'), None, None, 'tensor'), parts along dimension 0, may hold values from -6 to 6, as said below
- norm_gain: bfloat16 [16384], P('dp'), may hold values from 0.099609375 to 1.8984375
- w_query: bfloat16 [16384, 2048], P('dp', 'tensor'), may hold values from -1 to 1
- w_keyval: bfloat16 [16384, 2, 512], P('dp', None, 'tensor'), may hold values from -1 to 1, as said below
- w_out: bfloat16 [2048, 16384], P('tensor', 'dp'), may hold values from -0.125 to 0.125
Outputs:
- tree_features: bfloat16 [32, 4, 8, 16384], P('groups', None, None, ('dp', 'tensor')), parts along dimension 0
There are 2 independent parts, one for each index of `groups`. A program takes and returns all parts, laid end to end along the dimension named above; an argument that names none is the same for every part. Nothing has to cross between parts.
Inputs may be any that keep to these rules, and one draw needn't show every extreme that they name: `cache_lengths`: some request has exactly 512 valid cache positions and some other exactly 128. `cache_kv`: for each request, keys and values, the 4 blocks of 128 columns k * 4 .. (k + 1) * 4 - 1 are equal; they hold key-value head k. `w_keyval`: for keys and values, the 4 blocks of 128 columns k * 4 .. (k + 1) * 4 - 1 are equal; they hold key-value head k.
All inputs are finite; a program needn't handle non-finite values.
Results may differ from a plain program's by a relative error of at most 0.017.
Values may be sent and summed in bfloat16 or wider, within the bound.
A program may use at most 128 MiB of HBM per device.

v0:
```python
import jax
import jax.numpy as jnp
from jax import lax
from jax.sharding import PartitionSpec as P

D = 16384
HD = 128
BRANCH = 8
DEPTHS = 4
CACHE = 512


epsilon = 1e-05
masked_score = -1e30


def ancestor_path(parent_table, tree_level):
    current = jnp.broadcast_to(
        jnp.arange(BRANCH, dtype=jnp.int32)[None, :], (parent_table.shape[0], BRANCH)
    )
    path_nodes = [current]
    for upper in range(tree_level, 0, -1):
        current = jnp.take_along_axis(parent_table[:, upper - 1], current, axis=1)
        path_nodes.append(current)
    return path_nodes[::-1]


def tree_mask_of(parent_table, tree_level):
    path_nodes = ancestor_path(parent_table, tree_level)
    columns = jnp.arange(BRANCH, dtype=jnp.int32)
    blocks = []
    for other_level in range(DEPTHS):
        if other_level <= tree_level:
            blocks.append(columns[None, None, :] == path_nodes[other_level][:, :, None])
        else:
            blocks.append(jnp.zeros((parent_table.shape[0], BRANCH, BRANCH), dtype=bool))
    return jnp.concatenate(blocks, axis=2)


def shards(
    root_features,
    branch_embeds,
    parents,
    cache_lengths,
    cache_kv,
    norm_gain,
    w_query,
    w_keyval,
    w_out,
):
    request_count, feat_cols = root_features.shape
    local_requests = cache_lengths.shape[0]
    head_cols = w_query.shape[1]
    kv_cols = w_keyval.shape[2]
    kv_local = kv_cols // HD
    all_rows = request_count * BRANCH
    own_rows = local_requests * BRANCH
    share_cols = feat_cols // lax.axis_size("tensor")
    dp_index = lax.axis_index("dp")
    tensor_index = lax.axis_index("tensor")
    weights = jnp.concatenate([w_query, w_keyval.reshape(feat_cols, 2 * kv_cols)], axis=1)
    gain = norm_gain.astype(jnp.float32)
    own_parents = lax.dynamic_slice_in_dim(parents, dp_index * local_requests, local_requests, 0)
    cache_keys = cache_kv[:, 0].reshape(local_requests, CACHE, kv_local, HD)
    cache_values = cache_kv[:, 1].reshape(local_requests, CACHE, kv_local, HD)
    positions = jnp.arange(CACHE, dtype=jnp.int32)
    cache_valid = positions[None, :] < cache_lengths[:, None]
    tree_keys = jnp.zeros((local_requests, DEPTHS * BRANCH, kv_local, HD), jnp.bfloat16)
    tree_values = jnp.zeros((local_requests, DEPTHS * BRANCH, kv_local, HD), jnp.bfloat16)
    results = []
    previous = None
    for tree_level in range(DEPTHS):
        if tree_level == 0:
            parent = jnp.broadcast_to(root_features[:, None, :], (request_count, BRANCH, feat_cols))
        else:
            parent = jnp.take_along_axis(previous, parents[:, tree_level - 1][:, :, None], axis=1)
        node_state = parent.astype(jnp.float32) + branch_embeds[:, tree_level].astype(jnp.float32)
        flat_state = node_state.reshape(all_rows, feat_cols)
        square_sums = jnp.sum(flat_state * flat_state, axis=1)
        scaled = (flat_state * gain).astype(jnp.bfloat16)
        total_sums = lax.psum(square_sums, "dp")
        own_sums = lax.dynamic_slice_in_dim(total_sums, dp_index * own_rows, own_rows, 0)
        proj_terms = lax.psum_scatter(
            jnp.dot(scaled, weights, preferred_element_type=jnp.float32).astype(jnp.bfloat16),
            "dp",
            scatter_dimension=0,
            tiled=True,
        ).astype(jnp.float32)
        inv_rms = lax.rsqrt(own_sums / D + epsilon)[:, None]
        projected = (proj_terms * inv_rms).astype(jnp.bfloat16)
        queries = projected[:, :head_cols].reshape(local_requests, BRANCH, kv_local, -1, HD)
        new_keys = projected[:, head_cols : head_cols + kv_cols].reshape(
            local_requests, BRANCH, kv_local, HD
        )
        new_values = projected[:, head_cols + kv_cols :].reshape(
            local_requests, BRANCH, kv_local, HD
        )
        tree_keys = tree_keys.at[:, tree_level * BRANCH : (tree_level + 1) * BRANCH].set(new_keys)
        tree_values = tree_values.at[:, tree_level * BRANCH : (tree_level + 1) * BRANCH].set(
            new_values
        )
        tree_mask = tree_mask_of(own_parents, tree_level)
        cache_scores = jnp.einsum(
            "rbkgd,rckd->rkgbc", queries, cache_keys, preferred_element_type=jnp.float32
        ) * HD ** (-0.5)
        tree_scores = jnp.einsum(
            "rbkgd,rtkd->rkgbt", queries, tree_keys, preferred_element_type=jnp.float32
        ) * HD ** (-0.5)
        cache_scores = jnp.where(cache_valid[:, None, None, None, :], cache_scores, masked_score)
        tree_scores = jnp.where(tree_mask[:, None, None, :, :], tree_scores, masked_score)
        row_max = jnp.maximum(jnp.max(cache_scores, axis=4), jnp.max(tree_scores, axis=4))[
            ..., None
        ]
        cache_exp = jnp.exp(cache_scores - row_max)
        tree_exp = jnp.exp(tree_scores - row_max)
        denominator = jnp.sum(cache_exp, axis=4, keepdims=True) + jnp.sum(
            tree_exp, axis=4, keepdims=True
        )
        cache_weights = (cache_exp / denominator).astype(jnp.bfloat16)
        tree_weights = (tree_exp / denominator).astype(jnp.bfloat16)
        mixed = jnp.einsum(
            "rkgbc,rckd->rbkgd", cache_weights, cache_values, preferred_element_type=jnp.float32
        )
        mixed = mixed + jnp.einsum(
            "rkgbt,rtkd->rbkgd", tree_weights, tree_values, preferred_element_type=jnp.float32
        )
        attended = mixed.reshape(own_rows, head_cols).astype(jnp.bfloat16)
        partial_out = jnp.dot(
            lax.all_gather(attended, "dp", axis=0, tiled=True),
            w_out,
            preferred_element_type=jnp.float32,
        )
        share_sums = lax.psum_scatter(
            partial_out.astype(jnp.bfloat16), "tensor", scatter_dimension=1, tiled=True
        ).astype(jnp.float32)
        residual = lax.dynamic_slice_in_dim(flat_state, tensor_index * share_cols, share_cols, 1)
        fresh_share = (residual + share_sums).astype(jnp.bfloat16)
        if tree_level + 1 < DEPTHS:
            gathered = lax.all_gather(fresh_share, "tensor", axis=1, tiled=True)
            previous = gathered.reshape(request_count, BRANCH, feat_cols)
        results.append(fresh_share.reshape(request_count, BRANCH, share_cols))
    return jnp.stack(results, axis=1)


def solution(mesh):
    return jax.shard_map(
        shards,
        mesh=mesh,
        in_specs=(
            P("groups", "dp"),
            P("groups", None, None, "dp"),
            P("groups", None, None),
            P(("groups", "dp")),
            P(("groups", "dp"), None, None, "tensor"),
            P("dp"),
            P("dp", "tensor"),
            P("dp", None, "tensor"),
            P("tensor", "dp"),
        ),
        out_specs=P("groups", None, None, ("dp", "tensor")),
        check_vma=False,
    )
```

profile of v0, /device:TPU:0, one launch (start us, length us, event | category | flops | bytes accessed | tf_op | source)
XLA Modules:
  0.0 381.3 jit_solution(6987603568505349397)
XLA Ops:
  6.5 2.6 constant_dynamic-update-slice_fusion
  9.8 2.7 copy-done
  12.5 3.1 convolution_convert_fusion.7
  15.6 1.6 fusion.3
  17.5 0.8 gather_fusion.6
  18.4 8.4 %psum.28 = f32[128]{0:T(128)S(1)} all-reduce(f32[128]{0:T(128)S(1)} %reduce_sum.117), channel_id=1, replica_groups=mesh['groups'=2,'tensor'=4,'dp'=4] {'dp'}, use_global_device_ids=true, to_apply=%region_2.0 | all-reduce | flops 128 | bytes 1024 | tf_op jit(solution)/shard_map/psum | solution.py:81
  30.9 0.8 gather_fusion.8
  32.2 6.0 %reduce-scatter.9.cloned.1.call-done = bf16[32,768]{1,0:T(8,128)(2,1)} async-done(((bf16[128,768]{1,0:T(8,128)(2,1)}), bf16[32,768]{1,0:T(8,128)(2,1)}) %reduce-scatter.9.cloned.1.call-update) | async-done | bytes 49168 | tf_op jit(solution)/shard_map/reduce_scatter | solution.py:83
  38.2 0.9 multiply_convert_fusion.11
  40.6 5.4 %all_gather.21 = bf16[128,512]{1,0:T(8,128)(2,1)S(1)} all-gather(bf16[32,512]{1,0:T(8,128)(2,1)S(1)} %fusion.34), channel_id=1, replica_groups=mesh['groups'=2,'tensor'=4,'dp'=4] {'dp'}, dimensions={0}, use_global_device_ids=true | all-gather | bytes 163840 | tf_op jit(solution)/shard_map/all_gather | solution.py:129
  46.0 3.9 %convolution_convert_fusion.3 = bf16[128,4096]{1,0:T(8,128)(2,1)} fusion(bf16[128,512]{1,0:T(8,128)(2,1)S(1)} %all_gather.21, bf16[512,4096]{1,0:T(8,128)(2,1)} %param.37), kind=kOutput, calls=%fused_computation.12 | convolution fusion | flops 537395200 | bytes 5373952 | tf_op jit(solution)/shard_map/dot_general | solution.py:128
  50.0 1.4 fusion
  51.5 26.0 %reduce-scatter.11.cloned.1.call-done = bf16[128,1024]{1,0:T(8,128)(2,1)} async-done(((bf16[128,4096]{1,0:T(8,128)(2,1)}), bf16[128,1024]{1,0:T(8,128)(2,1)}) %reduce-scatter.11.cloned.1.call-update) | async-done | bytes 262160 | tf_op jit(solution)/shard_map/reduce_scatter | solution.py:133
  77.4 1.7 add_convert_fusion.3
  79.5 26.3 %all-gather.4.cloned.1.call-done = bf16[128,4096]{1,0:T(8,128)(2,1)} async-done(((bf16[128,1024]{1,0:T(8,128)(2,1)}), bf16[128,4096]{1,0:T(8,128)(2,1)}) %all-gather.4.cloned.1.call-update) | async-done | bytes 1048592 | tf_op jit(solution)/shard_map/all_gather | solution.py:139
  105.8 5.1 %gather_fusion = bf16[128,4096]{1,0:T(8,128)(2,1)} fusion(bf16[16,8,4096]{2,1,0:T(8,128)(2,1)} %bitcast.414, s32[128]{0:T(128)S(1)} %reshape.800), kind=kCustom, calls=%fused_computation.clone | custom fusion | bytes 2098176 | tf_op jit(solution)/shard_map/jit(take_along_axis)/gather | solution.py:76
  110.9 2.1 multiply_reduce_fusion.2
  113.0 4.5 %convolution_convert_fusion.6 = bf16[128,768]{1,0:T(8,128)(2,1)} fusion(bf16[4096,768]{1,0:T(8,128)(2,1)} %copy-done, f32[128,4096]{1,0:T(8,128)S(1)} %get-tuple-element.110, f32[4096]{0:T(1024)S(1)} %convert_element_type.206), kind=kOutput, calls=%fused_computation.35 | convolution fusion | flops 806453248 | bytes 8601600 | tf_op jit(solution)/shard_map/dot_general | solution.py:84
  117.7 6.1 %psum.29 = f32[128]{0:T(128)S(1)} all-reduce(f32[128]{0:T(128)S(1)} %reduce_sum.121), channel_id=1, replica_groups=mesh['groups'=2,'tensor'=4,'dp'=4] {'dp'}, use_global_device_ids=true, to_apply=%region_10.12 | all-reduce | flops 128 | bytes 1024 | tf_op jit(solution)/shard_map/psum | solution.py:81
  123.9 13.0 %reduce-scatter.13.cloned.1.call-done = bf16[32,768]{1,0:T(8,128)(2,1)} async-done(((bf16[128,768]{1,0:T(8,128)(2,1)}), bf16[32,768]{1,0:T(8,128)(2,1)}) %reduce-scatter.13.cloned.1.call-update) | async-done | bytes 49168 | tf_op jit(solution)/shard_map/reduce_scatter | solution.py:83
  136.8 0.9 multiply_convert_fusion.10
  139.2 5.4 %all_gather.23 = bf16[128,512]{1,0:T(8,128)(2,1)S(1)} all-gather(bf16[32,512]{1,0:T(8,128)(2,1)S(1)} %fusion.33), channel_id=1, replica_groups=mesh['groups'=2,'tensor'=4,'dp'=4] {'dp'}, dimensions={0}, use_global_device_ids=true | all-gather | bytes 163840 | tf_op jit(solution)/shard_map/all_gather | solution.py:129
  144.6 3.9 %convolution_convert_fusion.2 = bf16[128,4096]{1,0:T(8,128)(2,1)} fusion(bf16[128,512]{1,0:T(8,128)(2,1)S(1)} %all_gather.23, bf16[512,4096]{1,0:T(8,128)(2,1)} %param.37), kind=kOutput, calls=%fused_computation.11 | convolution fusion | flops 537395200 | bytes 5373952 | tf_op jit(solution)/shard_map/dot_general | solution.py:128
  148.6 27.4 %reduce-scatter.15.cloned.1.call-done = bf16[128,1024]{1,0:T(8,128)(2,1)} async-done(((bf16[128,4096]{1,0:T(8,128)(2,1)}), bf16[128,1024]{1,0:T(8,128)(2,1)}) %reduce-scatter.15.cloned.1.call-update) | async-done | bytes 262160 | tf_op jit(solution)/shard_map/reduce_scatter | solution.py:133
  176.0 1.7 add_convert_fusion.2
  178.2 26.2 %all-gather.6.cloned.1.call-done = bf16[128,4096]{1,0:T(8,128)(2,1)} async-done(((bf16[128,1024]{1,0:T(8,128)(2,1)}), bf16[128,4096]{1,0:T(8,128)(2,1)}) %all-gather.6.cloned.1.call-update) | async-done | bytes 1048592 | tf_op jit(solution)/shard_map/all_gather | solution.py:139
  204.4 4.8 %gather_fusion.2 = bf16[128,4096]{1,0:T(8,128)(2,1)} fusion(bf16[16,8,4096]{2,1,0:T(8,128)(2,1)} %bitcast.416, s32[128]{0:T(128)S(1)} %reshape.809), kind=kCustom, calls=%fused_computation.2.clone | custom fusion | bytes 2098176 | tf_op jit(solution)/shard_map/jit(take_along_axis)/gather | solution.py:76
  209.2 2.1 multiply_reduce_fusion.1
  211.3 4.5 %convolution_convert_fusion.5 = bf16[128,768]{1,0:T(8,128)(2,1)} fusion(bf16[4096,768]{1,0:T(8,128)(2,1)} %copy-done, f32[128,4096]{1,0:T(8,128)S(1)} %get-tuple-element.108, f32[4096]{0:T(1024)S(1)} %convert_element_type.206), kind=kOutput, calls=%fused_computation.34 | convolution fusion | flops 806453248 | bytes 8601600 | tf_op jit(solution)/shard_map/dot_general | solution.py:84
  215.9 6.1 %psum.30 = f32[128]{0:T(128)S(1)} all-reduce(f32[128]{0:T(128)S(1)} %reduce_sum.125), channel_id=1, replica_groups=mesh['groups'=2,'tensor'=4,'dp'=4] {'dp'}, use_global_device_ids=true, to_apply=%region_18.21 | all-reduce | flops 128 | bytes 1024 | tf_op jit(solution)/shard_map/psum | solution.py:81
  222.1 13.0 %reduce-scatter.17.cloned.1.call-done = bf16[32,768]{1,0:T(8,128)(2,1)} async-done(((bf16[128,768]{1,0:T(8,128)(2,1)}), bf16[32,768]{1,0:T(8,128)(2,1)}) %reduce-scatter.17.cloned.1.call-update) | async-done | bytes 49168 | tf_op jit(solution)/shard_map/reduce_scatter | solution.py:83
  235.2 0.9 multiply_convert_fusion.9
  237.5 5.4 %all_gather.25 = bf16[128,512]{1,0:T(8,128)(2,1)S(1)} all-gather(bf16[32,512]{1,0:T(8,128)(2,1)S(1)} %fusion.32), channel_id=1, replica_groups=mesh['groups'=2,'tensor'=4,'dp'=4] {'dp'}, dimensions={0}, use_global_device_ids=true | all-gather | bytes 163840 | tf_op jit(solution)/shard_map/all_gather | solution.py:129
  243.0 3.9 %convolution_convert_fusion.1 = bf16[128,4096]{1,0:T(8,128)(2,1)} fusion(bf16[128,512]{1,0:T(8,128)(2,1)S(1)} %all_gather.25, bf16[512,4096]{1,0:T(8,128)(2,1)} %param.37), kind=kOutput, calls=%fused_computation.10 | convolution fusion | flops 537395200 | bytes 5373952 | tf_op jit(solution)/shard_map/dot_general | solution.py:128
  247.0 27.4 %reduce-scatter.19.cloned.1.call-done = bf16[128,1024]{1,0:T(8,128)(2,1)} async-done(((bf16[128,4096]{1,0:T(8,128)(2,1)}), bf16[128,1024]{1,0:T(8,128)(2,1)}) %reduce-scatter.19.cloned.1.call-update) | async-done | bytes 262160 | tf_op jit(solution)/shard_map/reduce_scatter | solution.py:133
  274.4 1.7 add_convert_fusion.1
  276.4 26.3 %all-gather.8.cloned.1.call-done = bf16[128,4096]{1,0:T(8,128)(2,1)} async-done(((bf16[128,1024]{1,0:T(8,128)(2,1)}), bf16[128,4096]{1,0:T(8,128)(2,1)}) %all-gather.8.cloned.1.call-update) | async-done | bytes 1048592 | tf_op jit(solution)/shard_map/all_gather | solution.py:139
  302.7 4.8 %gather_fusion.5 = bf16[128,4096]{1,0:T(8,128)(2,1)} fusion(bf16[16,8,4096]{2,1,0:T(8,128)(2,1)} %bitcast.415, s32[128]{0:T(128)S(1)} %reshape.823), kind=kCustom, calls=%fused_computation.3.clone | custom fusion | bytes 2098176 | tf_op jit(solution)/shard_map/jit(take_along_axis)/gather | solution.py:76
  307.6 2.1 multiply_reduce_fusion
  309.7 4.5 %convolution_convert_fusion.4 = bf16[128,768]{1,0:T(8,128)(2,1)} fusion(bf16[4096,768]{1,0:T(8,128)(2,1)} %copy-done, f32[128,4096]{1,0:T(8,128)S(1)} %get-tuple-element.106, f32[4096]{0:T(1024)S(1)} %convert_element_type.206), kind=kOutput, calls=%fused_computation.33 | convolution fusion | flops 806453248 | bytes 8601600 | tf_op jit(solution)/shard_map/dot_general | solution.py:84
  314.3 6.1 %psum.31 = f32[128]{0:T(128)S(1)} all-reduce(f32[128]{0:T(128)S(1)} %reduce_sum.129), channel_id=1, replica_groups=mesh['groups'=2,'tensor'=4,'dp'=4] {'dp'}, use_global_device_ids=true, to_apply=%region_26.29 | all-reduce | flops 128 | bytes 1024 | tf_op jit(solution)/shard_map/psum | solution.py:81
  320.4 13.0 %reduce-scatter.21.cloned.1.call-done = bf16[32,768]{1,0:T(8,128)(2,1)} async-done(((bf16[128,768]{1,0:T(8,128)(2,1)}), bf16[32,768]{1,0:T(8,128)(2,1)}) %reduce-scatter.21.cloned.1.call-update) | async-done | bytes 49168 | tf_op jit(solution)/shard_map/reduce_scatter | solution.py:83
  333.5 0.9 multiply_convert_fusion.8
  335.9 5.4 %all_gather.27 = bf16[128,512]{1,0:T(8,128)(2,1)S(1)} all-gather(bf16[32,512]{1,0:T(8,128)(2,1)S(1)} %fusion.31), channel_id=1, replica_groups=mesh['groups'=2,'tensor'=4,'dp'=4] {'dp'}, dimensions={0}, use_global_device_ids=true | all-gather | bytes 163840 | tf_op jit(solution)/shard_map/all_gather | solution.py:129
  341.3 3.9 %convolution_convert_fusion = bf16[128,4096]{1,0:T(8,128)(2,1)} fusion(bf16[128,512]{1,0:T(8,128)(2,1)S(1)} %all_gather.27, bf16[512,4096]{1,0:T(8,128)(2,1)} %param.37), kind=kOutput, calls=%fused_computation.9 | convolution fusion | flops 537395200 | bytes 5373952 | tf_op jit(solution)/shard_map/dot_general | solution.py:128
  345.2 27.4 %reduce-scatter.23.cloned.1.call-done = bf16[128,1024]{1,0:T(8,128)(2,1)} async-done(((bf16[128,4096]{1,0:T(8,128)(2,1)}), bf16[128,1024]{1,0:T(8,128)(2,1)}) %reduce-scatter.23.cloned.1.call-update) | async-done | bytes 262160 | tf_op jit(solution)/shard_map/reduce_scatter | solution.py:133
  372.6 1.0 fusion.55
  373.7 1.1 pad_maximum_fusion
  (136 shorter events, 13.6 us)
Async XLA Ops:
  6.5 2.6 copy-start.8
  6.5 2.6 copy-start.6
  6.5 2.9 copy-start.5
  6.5 31.7 %reduce-scatter.9.cloned.1.call-start = ((), (), s32[]{:S(2)}) async-start(), calls=%async_computation.8 | async-start | bytes 245760 | tf_op jit(solution)/shard_map/reduce_scatter | solution.py:83
  9.8 2.7 copy-start
  12.5 4.7 %copy-start.7 = (s32[16,3,8]{0,2,1:T(8,128)S(1)}, s32[16,3,8]{0,2,1:T(8,128)}, u32[]{:S(2)}) copy-start(s32[16,3,8]{0,2,1:T(8,128)} %param.31) | copy-start | bytes 4612
  15.6 61.9 %reduce-scatter.11.cloned.1.call-start = ((), (), s32[]{:S(2)}) async-start(), calls=%async_computation.9 | async-start | bytes 1310720 | tf_op jit(solution)/shard_map/reduce_scatter | solution.py:133
  29.6 2.4 copy-start.9
  29.6 9.5 %copy-start.1 = (bf16[4,2,512,128]{3,2,1,0:T(8,128)(2,1)S(1)}, bf16[4,2,512,128]{3,2,1,0:T(8,128)(2,1)}, u32[]{:S(2)}) copy-start(bf16[4,2,512,128]{3,2,1,0:T(8,128)(2,1)} %param.33) | copy-start | bytes 3145732
  50.0 55.8 %all-gather.4.cloned.1.call-start = ((), (), s32[]{:S(2)}) async-start(), calls=%async_computation.10 | async-start | bytes 1310720 | tf_op jit(solution)/shard_map/all_gather | solution.py:139
  79.2 57.6 %reduce-scatter.13.cloned.1.call-start = ((), (), s32[]{:S(2)}) async-start(), calls=%async_computation.11 | async-start | bytes 245760 | tf_op jit(solution)/shard_map/reduce_scatter | solution.py:83
  117.5 58.5 %reduce-scatter.15.cloned.1.call-start = ((), (), s32[]{:S(2)}) async-start(), calls=%async_computation.12 | async-start | bytes 1310720 | tf_op jit(solution)/shard_map/reduce_scatter | solution.py:133
  148.6 55.8 %all-gather.6.cloned.1.call-start = ((), (), s32[]{:S(2)}) async-start(), calls=%async_computation.13 | async-start | bytes 1310720 | tf_op jit(solution)/shard_map/all_gather | solution.py:139
  177.7 57.4 %reduce-scatter.17.cloned.1.call-start = ((), (), s32[]{:S(2)}) async-start(), calls=%async_computation.14 | async-start | bytes 245760 | tf_op jit(solution)/shard_map/reduce_scatter | solution.py:83
  215.8 58.6 %reduce-scatter.19.cloned.1.call-start = ((), (), s32[]{:S(2)}) async-start(), calls=%async_computation.15 | async-start | bytes 1310720 | tf_op jit(solution)/shard_map/reduce_scatter | solution.py:133
  246.9 55.8 %all-gather.8.cloned.1.call-start = ((), (), s32[]{:S(2)}) async-start(), calls=%async_computation.16 | async-start | bytes 1310720 | tf_op jit(solution)/shard_map/all_gather | solution.py:139
  276.1 57.4 %reduce-scatter.21.cloned.1.call-start = ((), (), s32[]{:S(2)}) async-start(), calls=%async_computation.17 | async-start | bytes 245760 | tf_op jit(solution)/shard_map/reduce_scatter | solution.py:83
  314.1 58.5 %reduce-scatter.23.cloned.1.call-start = ((), (), s32[]{:S(2)}) async-start(), calls=%async_computation.18 | async-start | bytes 1310720 | tf_op jit(solution)/shard_map/reduce_scatter | solution.py:133
  345.2 28.5 %copy-start.2 = (bf16[128,1024]{1,0:T(8,128)(2,1)S(1)}, bf16[128,1024]{1,0:T(8,128)(2,1)}, u32[]{:S(2)}) copy-start(bf16[128,1024]{1,0:T(8,128)(2,1)} %add_convert_fusion.3) | copy-start | bytes 786436
  345.2 28.5 %copy-start.3 = (bf16[128,1024]{1,0:T(8,128)(2,1)S(1)}, bf16[128,1024]{1,0:T(8,128)(2,1)}, u32[]{:S(2)}) copy-start(bf16[128,1024]{1,0:T(8,128)(2,1)} %add_convert_fusion.2) | copy-start | bytes 786436
  345.2 28.5 %copy-start.4 = (bf16[128,1024]{1,0:T(8,128)(2,1)S(1)}, bf16[128,1024]{1,0:T(8,128)(2,1)}, u32[]{:S(2)}) copy-start(bf16[128,1024]{1,0:T(8,128)(2,1)} %add_convert_fusion.1) | copy-start | bytes 786436
Sparse Core Ops, SparseCore 0:
  15.7 22.4 reduce-scatter.8
  50.1 27.3 reduce-scatter.10
  79.3 26.4 all-gather.3
  117.6 19.1 reduce-scatter.12
  148.7 27.2 reduce-scatter.14
  177.9 26.4 all-gather.5
  215.9 19.1 reduce-scatter.16
  247.0 27.2 reduce-scatter.18
  276.2 26.4 all-gather.7
  314.3 19.1 reduce-scatter.20
  345.3 27.2 reduce-scatter.22
where the time goes:
time: 383 us; the launch traced here: 381 us
  waiting for transfers between devices  232 us (61%)
  blocking collectives  48.3 us (13%)
  matrix products  36.4 us (10%)
  local copies, waits for them, and re-layouts  27.6 us (7%)
  other arithmetic  22.6 us (6%)
  between operations  13.6 us (4%)
    reduce_scatter x4, waiting for transfers between devices, shards(): lax.psum_scatter(partial_out.astype(jnp.bfloat16), 'tensor', scatter_dime...  108 us
    all_gather x3, waiting for transfers between devices, shards(): gathered = lax.all_gather(fresh_share, 'tensor', axis=1, tiled=True)  78.8 us
    reduce_scatter x4, waiting for transfers between devices, shards(): lax.psum_scatter(jnp.dot(scaled, weights, preferred_element_type=jnp.floa...  45.1 us
    psum x4, blocking collectives, shards(): total_sums = lax.psum(square_sums, 'dp')  26.6 us
    all_gather x4, blocking collectives, shards(): lax.all_gather(attended, 'dp', axis=0, tiled=True)  21.7 us
    dot_general x4, matrix products, shards(): jnp.dot(scaled, weights, preferred_element_type=jnp.float32)  16.4 us
    dot_general x4, matrix products, shards(): jnp.dot(lax.all_gather(attended, 'dp', axis=0, tiled=True), w_out, prefer...  15.7 us
    gather x9, local copies, waits for them, and re-layouts, shards(): jnp.take_along_axis(previous, parents[:, tree_level - 1][:, :, None], axi...  15.3 us
  transfers between devices with their start and end apart: 11, of which 11 were waited for; matrix products, arithmetic and copies ran while one was open for 3% of the time, Pallas kernels for 0%

commit v1 on v0

--- a/solution.py
+++ b/solution.py
@@ -1,6 +1,10 @@
+import functools
+
 import jax
 import jax.numpy as jnp
 from jax import lax
+from jax.experimental import pallas as pl
+from jax.experimental.pallas import tpu as pltpu
 from jax.sharding import PartitionSpec as P
 
 D = 16384
@@ -142,9 +146,560 @@
     return jnp.stack(results, axis=1)
 
 
+MESH = pl.DeviceIdType.MESH
+
+
+def dot32(a, b):
+    return jnp.dot(a, b, preferred_element_type=jnp.float32)
+
+
+def dot32_t(a, b):
+    return lax.dot_general(a, b, (((1,), (1,)), ((), ())), preferred_element_type=jnp.float32)
+
+
+def tree_kernel(
+    n,
+    m,
+    root_ref,
+    emb_hbm,
+    hot_ref,
+    own_hot_ref,
+    len_ref,
+    cache_hbm,
+    gain_ref,
+    wq_hbm,
+    wkv_hbm,
+    wo_hbm,
+    out_ref,
+    emb0,
+    emb_share,
+    cache,
+    wq,
+    wkv,
+    wo,
+    scaled,
+    share_sums,
+    state,
+    proj,
+    proj_send,
+    proj_recv,
+    sums_send,
+    sums_recv,
+    tree_keys,
+    tree_values,
+    tree_mask,
+    att,
+    part,
+    rs_send,
+    rs_recv,
+    total,
+    load_sem,
+    ag_ssem,
+    ag_rsem,
+    tsum_ssem,
+    tsum_rsem,
+    proj_ssem,
+    proj_rsem,
+    dsum_ssem,
+    dsum_rsem,
+    att_ssem,
+    att_rsem,
+    rs_ssem,
+    rs_rsem,
+):
+    t = lax.axis_index("tensor")
+    d = lax.axis_index("dp")
+    requests, feat = root_ref.shape
+    rows = requests * BRANCH
+    own = rows // m
+    own_requests = requests // m
+    share = feat // n
+    head_cols = wq.shape[1]
+    heads = head_cols // HD
+
+    def cols_of(s):
+        return pl.ds(pl.multiple_of(s * share, share), share)
+
+    loads = [
+        pltpu.make_async_copy(emb_hbm.at[:, 0], emb0, load_sem.at[0]),
+        pltpu.make_async_copy(wq_hbm, wq, load_sem.at[1]),
+        pltpu.make_async_copy(wkv_hbm, wkv, load_sem.at[2]),
+        pltpu.make_async_copy(cache_hbm, cache, load_sem.at[3]),
+        pltpu.make_async_copy(wo_hbm, wo, load_sem.at[4]),
+    ]
+    for e in range(1, DEPTHS):
+        loads.append(
+            pltpu.make_async_copy(
+                emb_hbm.at[:, e, :, cols_of(t)], emb_share.at[e - 1], load_sem.at[4 + e]
+            )
+        )
+    for load in loads:
+        load.start()
+
+    dp_to = [lax.rem(d + k, m) for k in range(1, m)]
+    t_to = [lax.rem(t + k, n) for k in range(1, n)]
+
+    barrier = pltpu.get_barrier_semaphore()
+    for peer in dp_to:
+        pl.semaphore_signal(barrier, inc=1, device_id={"dp": peer}, device_id_type=MESH)
+    for peer in t_to:
+        pl.semaphore_signal(barrier, inc=1, device_id={"tensor": peer}, device_id_type=MESH)
+    pl.semaphore_wait(barrier, m + n - 2)
+
+    def ag_copy(e, s, to, send_slot):
+        return pltpu.make_async_remote_copy(
+            src_ref=scaled.at[e, s],
+            dst_ref=scaled.at[e, s],
+            send_sem=ag_ssem.at[e, send_slot],
+            recv_sem=ag_rsem.at[e, s],
+            device_id={"tensor": to},
+            device_id_type=MESH,
+        )
+
+    def tsum_copy(e, k):
+        return pltpu.make_async_remote_copy(
+            src_ref=share_sums.at[e, n - 1],
+            dst_ref=share_sums.at[e, k],
+            send_sem=tsum_ssem.at[e, k],
+            recv_sem=tsum_rsem.at[e, k],
+            device_id={"tensor": t_to[k]},
+            device_id_type=MESH,
+        )
+
+    def proj_copy(e, k):
+        return pltpu.make_async_remote_copy(
+            src_ref=proj_send.at[e, dp_to[k]],
+            dst_ref=proj_recv.at[e, k],
+            send_sem=proj_ssem.at[e, k],
+            recv_sem=proj_rsem.at[e, k],
+            device_id={"dp": dp_to[k]},
+            device_id_type=MESH,
+        )
+
+    def dsum_copy(e, k):
+        return pltpu.make_async_remote_copy(
+            src_ref=sums_send.at[e],
+            dst_ref=sums_recv.at[e, k],
+            send_sem=dsum_ssem.at[e, k],
+            recv_sem=dsum_rsem.at[e, k],
+            device_id={"dp": dp_to[k]},
+            device_id_type=MESH,
+        )
+
+    def att_copy(e, k):
+        return pltpu.make_async_remote_copy(
+            src_ref=att.at[e, d],
+            dst_ref=att.at[e, d],
+            send_sem=att_ssem.at[e, k],
+            recv_sem=att_rsem.at[e, k],
+            device_id={"dp": dp_to[k]},
+            device_id_type=MESH,
+        )
+
+    def rs_copy(e, s, to, slot):
+        return pltpu.make_async_remote_copy(
+            src_ref=rs_send.at[e, s],
+            dst_ref=rs_recv.at[e, slot],
+            send_sem=rs_ssem.at[e, s],
+            recv_sem=rs_rsem.at[e, slot],
+            device_id={"tensor": to},
+            device_id_type=MESH,
+        )
+
+    def rs_right(e, s):
+        return rs_copy(e, s, t + 1, s)
+
+    def rs_left(e, s):
+        return rs_copy(e, s, t - 1, jnp.where(t - 1 == s, n, s))
+
+    def rs_wait(e, slot):
+        rs_copy(e, 0, lax.rem(t + 1, n), slot).wait_recv()
+
+    row_id = lax.broadcasted_iota(jnp.int32, (rows, rows), 0)
+    col_id = lax.broadcasted_iota(jnp.int32, (rows, rows), 1)
+    eye = row_id == col_id
+
+    def to_lanes(column):
+        spread = jnp.where(eye, jnp.broadcast_to(column, (rows, rows)), 0.0)
+        return jnp.broadcast_to(jnp.sum(spread, axis=0, keepdims=True), (8, rows))
+
+    spread_id = lax.broadcasted_iota(jnp.int32, (rows, requests), 0) // BRANCH
+    root_hot = (
+        spread_id == lax.broadcasted_iota(jnp.int32, (rows, requests), 1)
+    ).astype(jnp.bfloat16)
+    loads[0].wait()
+    squares = jnp.zeros((rows, 1), jnp.float32)
+    for s in range(n):
+        cols = slice(s * share, (s + 1) * share)
+        node = dot32(root_hot, root_ref[:, cols]) + emb0[:, :, cols].astype(jnp.float32).reshape(
+            rows, share
+        )
+        squares = squares + jnp.sum(node * node, axis=1, keepdims=True)
+        scaled[0, s] = (node * gain_ref[:, cols]).astype(jnp.bfloat16)
+
+        @pl.when(t == s)
+        def _():
+            state[...] = node
+
+    sums_send[0] = to_lanes(squares)
+    tree_keys[...] = jnp.zeros_like(tree_keys)
+    tree_values[...] = jnp.zeros_like(tree_values)
+    tree_mask[...] = jnp.zeros_like(tree_mask)
+    for load in loads[1:]:
+        load.wait()
+
+    def level(e, carry):
+        def product(s):
+            block = scaled[e, s]
+            proj[:, :head_cols] += dot32(block, wq[cols_of(s)])
+            proj[:, head_cols:] += dot32(block, wkv[cols_of(s)])
+
+        proj[...] = jnp.zeros_like(proj)
+        product(t)
+
+        for k in range(1, n):
+            before = t - k
+            after = t + k
+
+            @pl.when((before >= 0) & (e > 0))
+            def _():
+                ag_copy(e, before, lax.rem(t + 1, n), before).wait_recv()
+
+                @pl.when(t < n - 1)
+                def _():
+                    ag_copy(e, before, t + 1, before).start()
+
+            @pl.when((after < n) & (e > 0))
+            def _():
+                ag_copy(e, after, lax.rem(t + 1, n), after).wait_recv()
+
+                @pl.when(t > 0)
+                def _():
+                    ag_copy(e, after, t - 1, after).start()
+
+            @pl.when(before >= 0)
+            def _():
+                product(before)
+
+            @pl.when(after < n)
+            def _():
+                product(after)
+
+        @pl.when(e > 0)
+        def _():
+            summed = share_sums[e, n - 1]
+            for k in range(n - 1):
+                tsum_copy(e, k).wait_recv()
+                summed = summed + share_sums[e, k]
+            sums_send[e] = summed
+
+        for k in range(m):
+            proj_send[e, k] = proj[k * own : (k + 1) * own].astype(jnp.bfloat16)
+        for k in range(m - 1):
+            proj_copy(e, k).start()
+            dsum_copy(e, k).start()
+
+        own_row = lax.broadcasted_iota(jnp.int32, (own, DEPTHS * own), 0)
+        own_col = lax.broadcasted_iota(jnp.int32, (own, DEPTHS * own), 1)
+        itself = (own_col == own_row + e * own).astype(jnp.float32)
+        above = dot32(own_hot_ref[e], tree_mask[...])
+        mask_now = itself + above
+        tree_mask[...] = mask_now.astype(jnp.bfloat16)
+
+        projected = proj[pl.ds(pl.multiple_of(d * own, own), own)]
+        summed = sums_send[e]
+        for k in range(m - 1):
+            proj_copy(e, k).wait_recv()
+            dsum_copy(e, k).wait_recv()
+            projected = projected + proj_recv[e, k].astype(jnp.float32)
+            summed = summed + sums_recv[e, k]
+        pick = lax.broadcasted_iota(jnp.int32, (own, rows), 1) == (
+            lax.broadcasted_iota(jnp.int32, (own, rows), 0) + d * own
+        )
+        own_sums = jnp.sum(
+            jnp.where(pick, jnp.broadcast_to(summed[0:1], (own, rows)), 0.0),
+            axis=1,
+            keepdims=True,
+        )
+        inv_rms = lax.rsqrt(own_sums / (feat * m) + epsilon)
+        projected = projected * inv_rms
+        queries = jnp.concatenate(
+            [
+                projected[:, h * HD : (h + 1) * HD].reshape(own_requests, 1, BRANCH, HD)
+                for h in range(heads)
+            ],
+            axis=1,
+        ).reshape(own * heads, HD).astype(jnp.bfloat16)
+        now = pl.ds(pl.multiple_of(e * own, own), own)
+        tree_keys[now] = projected[:, head_cols : head_cols + HD].astype(jnp.bfloat16)
+        tree_values[now] = projected[:, head_cols + HD :].astype(jnp.bfloat16)
+
+        per = heads * BRANCH
+        tree_scores = dot32_t(queries, tree_keys[...]) * HD ** (-0.5)
+        allowed = jnp.broadcast_to(
+            mask_now.reshape(own_requests, 1, BRANCH, DEPTHS * own),
+            (own_requests, heads, BRANCH, DEPTHS * own),
+        ).reshape(own * heads, DEPTHS * own)
+        tree_scores = jnp.where(allowed > 0.5, tree_scores, masked_score)
+        cache_scores = []
+        position = lax.broadcasted_iota(jnp.int32, (per, CACHE), 1)
+        for r in range(own_requests):
+            scores = dot32_t(queries[r * per : (r + 1) * per], cache[r, 0]) * HD ** (-0.5)
+            cache_scores.append(jnp.where(position < len_ref[r], scores, masked_score))
+        cache_scores = jnp.concatenate(cache_scores, axis=0)
+        row_max = jnp.maximum(
+            jnp.max(cache_scores, axis=1, keepdims=True),
+            jnp.max(tree_scores, axis=1, keepdims=True),
+        )
+        cache_exp = jnp.exp(cache_scores - row_max)
+        tree_exp = jnp.exp(tree_scores - row_max)
+        denominator = jnp.sum(cache_exp, axis=1, keepdims=True) + jnp.sum(
+            tree_exp, axis=1, keepdims=True
+        )
+        cache_weights = (cache_exp / denominator).astype(jnp.bfloat16)
+        tree_weights = (tree_exp / denominator).astype(jnp.bfloat16)
+        mixed = jnp.concatenate(
+            [
+                dot32(cache_weights[r * per : (r + 1) * per], cache[r, 1])
+                for r in range(own_requests)
+            ],
+            axis=0,
+        ) + dot32(tree_weights, tree_values[...])
+        mixed = mixed.reshape(own_requests, heads, BRANCH, HD)
+        for h in range(heads):
+            att[e, d, :, h * HD : (h + 1) * HD] = mixed[:, h].reshape(own, HD).astype(jnp.bfloat16)
+        for k in range(m - 1):
+            att_copy(e, k).start()
+        for k in range(m - 1):
+            att_copy(e, k).wait_recv()
+
+        attended = att[e].reshape(rows, head_cols)
+
+        def own_part(s):
+            part[s] = dot32(attended, wo[:, s * share : (s + 1) * share])
+
+        done = set()
+        for k in range(n - 1):
+            right, left = n - 1 - k, k
+            for s in (right, left):
+                if s not in done:
+                    own_part(s)
+                    done.add(s)
+
+            @pl.when(t == 0)
+            def _():
+                rs_send[e, right] = part[right].astype(jnp.bfloat16)
+                rs_right(e, right).start()
+
+            @pl.when(t == n - 1)
+            def _():
+                rs_send[e, left] = part[left].astype(jnp.bfloat16)
+                rs_left(e, left).start()
+
+        def relay_right(s):
+            @pl.when((t > 0) & (t < s))
+            def _():
+                rs_wait(e, s)
+                rs_send[e, s] = (part[s] + rs_recv[e, s].astype(jnp.float32)).astype(jnp.bfloat16)
+                rs_right(e, s).start()
+
+        def relay_left(s):
+            @pl.when((t < n - 1) & (t > s))
+            def _():
+                rs_wait(e, s)
+                rs_send[e, s] = (part[s] + rs_recv[e, s].astype(jnp.float32)).astype(jnp.bfloat16)
+                rs_left(e, s).start()
+
+        @pl.when(t < n // 2)
+        def _():
+            for k in range(n - 1):
+                relay_right(n - 1 - k)
+                relay_left(k)
+
+        @pl.when(t >= n // 2)
+        def _():
+            for k in range(n - 1):
+                relay_left(k)
+                relay_right(n - 1 - k)
+
+        total[...] = state[...] + part[t]
+
+        @pl.when(t > 0)
+        def _():
+            rs_wait(e, t)
+            total[...] += rs_recv[e, t].astype(jnp.float32)
+
+        @pl.when(t < n - 1)
+        def _():
+            rs_wait(e, n)
+            total[...] += rs_recv[e, n].astype(jnp.float32)
+
+        fresh = total[...]
+        out_ref[:, pl.ds(e, 1)] = fresh.reshape(requests, 1, BRANCH, share).astype(jnp.bfloat16)
+
+        @pl.when(e < DEPTHS - 1)
+        def _():
+            node = dot32(hot_ref[e], fresh.astype(jnp.bfloat16)) + emb_share[e].astype(
+                jnp.float32
+            ).reshape(rows, share)
+            state[...] = node
+            scaled[e + 1, t] = (node * gain_ref[:, cols_of(t)]).astype(jnp.bfloat16)
+
+            @pl.when(t < n - 1)
+            def _():
+                ag_copy(e + 1, t, t + 1, t).start()
+
+            @pl.when(t > 0)
+            def _():
+                ag_copy(e + 1, t, t - 1, n).start()
+
+            share_sums[e + 1, n - 1] = to_lanes(jnp.sum(node * node, axis=1, keepdims=True))
+            for k in range(n - 1):
+                tsum_copy(e + 1, k).start()
+
+        return carry
+
+    lax.fori_loop(0, DEPTHS, level, 0)
+
+    def drain(e, carry):
+        for k in range(m - 1):
+            proj_copy(e, k).wait_send()
+            dsum_copy(e, k).wait_send()
+            att_copy(e, k).wait_send()
+        for s in range(n):
+
+            @pl.when(t < s)
+            def _():
+                rs_right(e, s).wait_send()
+
+            @pl.when(t > s)
+            def _():
+                rs_left(e, s).wait_send()
+
+        @pl.when(e > 0)
+        def _():
+            for k in range(n - 1):
+                tsum_copy(e, k).wait_send()
+            for s in range(n):
+
+                @pl.when((s <= t) & (t < n - 1))
+                def _():
+                    ag_copy(e, s, t + 1, s).wait_send()
+
+                @pl.when((s > t) & (t > 0))
+                def _():
+                    ag_copy(e, s, t - 1, s).wait_send()
+
+            @pl.when(t > 0)
+            def _():
+                ag_copy(e, t, t - 1, n).wait_send()
+
+        return carry
+
+    lax.fori_loop(0, DEPTHS, drain, 0)
+
+
+def kernel_shards(
+    root_features,
+    branch_embeds,
+    parents,
+    cache_lengths,
+    cache_kv,
+    norm_gain,
+    w_query,
+    w_keyval,
+    w_out,
+):
+    n = lax.axis_size("tensor")
+    m = lax.axis_size("dp")
+    requests, feat = root_features.shape
+    own_requests = cache_lengths.shape[0]
+    rows = requests * BRANCH
+    own = own_requests * BRANCH
+    share = feat // n
+    head_cols = w_query.shape[1]
+    proj_cols = head_cols + 2 * HD
+
+    def one_hots(table):
+        count = table.shape[0]
+        first = (jnp.arange(count, dtype=jnp.int32) * BRANCH)[None, :, None]
+        index = (jnp.swapaxes(table, 0, 1) + first).reshape(DEPTHS - 1, count * BRANCH)
+        lane = jnp.arange(count * BRANCH, dtype=jnp.int32)
+        return (index[:, :, None] == lane[None, None, :]).astype(jnp.bfloat16)
+
+    hot = one_hots(parents)
+    own_parents = lax.dynamic_slice_in_dim(
+        parents, lax.axis_index("dp") * own_requests, own_requests, 0
+    )
+    own_hot = jnp.pad(one_hots(own_parents), ((1, 0), (0, 0), (0, 0)))
+    bf16, f32 = jnp.bfloat16, jnp.float32
+    vmem = pl.BlockSpec(memory_space=pltpu.VMEM)
+    smem = pl.BlockSpec(memory_space=pltpu.SMEM)
+    hbm = pl.BlockSpec(memory_space=pl.ANY)
+    dma = pltpu.SemaphoreType.DMA
+    return pl.pallas_call(
+        functools.partial(tree_kernel, n, m),
+        out_shape=jax.ShapeDtypeStruct((requests, DEPTHS, BRANCH, share), bf16),
+        in_specs=[vmem, hbm, vmem, vmem, smem, hbm, vmem, hbm, hbm, hbm],
+        out_specs=vmem,
+        scratch_shapes=[
+            pltpu.VMEM((requests, BRANCH, feat), bf16),
+            pltpu.VMEM((DEPTHS - 1, requests, BRANCH, share), bf16),
+            pltpu.VMEM(cache_kv.shape, bf16),
+            pltpu.VMEM((feat, head_cols), bf16),
+            pltpu.VMEM((feat, 2 * HD), bf16),
+            pltpu.VMEM((head_cols, feat), bf16),
+            pltpu.VMEM((DEPTHS, n, rows, share), bf16),
+            pltpu.VMEM((DEPTHS, n, 8, rows), f32),
+            pltpu.VMEM((rows, share), f32),
+            pltpu.VMEM((rows, proj_cols), f32),
+            pltpu.VMEM((DEPTHS, m, own, proj_cols), bf16),
+            pltpu.VMEM((DEPTHS, m - 1, own, proj_cols), bf16),
+            pltpu.VMEM((DEPTHS, 8, rows), f32),
+            pltpu.VMEM((DEPTHS, m - 1, 8, rows), f32),
+            pltpu.VMEM((DEPTHS * own, HD), bf16),
+            pltpu.VMEM((DEPTHS * own, HD), bf16),
+            pltpu.VMEM((own, DEPTHS * own), bf16),
+            pltpu.VMEM((DEPTHS, m, own, head_cols), bf16),
+            pltpu.VMEM((n, rows, share), f32),
+            pltpu.VMEM((DEPTHS, n, rows, share), bf16),
+            pltpu.VMEM((DEPTHS, n + 1, rows, share), bf16),
+            pltpu.VMEM((rows, share), f32),
+            dma((4 + DEPTHS,)),
+            dma((DEPTHS, n + 1)),
+            dma((DEPTHS, n)),
+            dma((DEPTHS, n - 1)),
+            dma((DEPTHS, n - 1)),
+            dma((DEPTHS, m - 1)),
+            dma((DEPTHS, m - 1)),
+            dma((DEPTHS, m - 1)),
+            dma((DEPTHS, m - 1)),
+            dma((DEPTHS, m - 1)),
+            dma((DEPTHS, m - 1)),
+            dma((DEPTHS, n)),
+            dma((DEPTHS, n + 1)),
+        ],
+        compiler_params=pltpu.CompilerParams(
+            collective_id=0, has_side_effects=True, vmem_limit_bytes=60 * 1024 * 1024
+        ),
+    )(
+        root_features,
+        branch_embeds,
+        hot,
+        own_hot,
+        cache_lengths,
+        cache_kv,
+        norm_gain.astype(f32)[None, :],
+        w_query,
+        w_keyval.reshape(feat, 2 * HD),
+        w_out,
+    )
+
+
 def solution(mesh):
+    in_line = 1 < mesh.shape["tensor"] <= 8 and mesh.shape["dp"] > 1
     return jax.shard_map(
-        shards,
+        kernel_shards if in_line else shards,
         mesh=mesh,
         in_specs=(
             P("groups", "dp"),

time: 383 us -> 195 us (0.51)
  waiting for transfers between devices: 232 us -> 0 us
  Pallas kernels: 0 us -> 184 us
  blocking collectives: 48.3 us -> 0 us
  matrix products: 36.4 us -> 0 us
  local copies, waits for them, and re-layouts: 27.6 us -> 5.85 us
  other arithmetic: 22.6 us -> 4.26 us
  between operations: 13.6 us -> 0.02 us
    pallas_call x0 -> x1, Pallas kernels: none -> 184 us  [kernel_shards(): pl.pallas_call(functools.partial(tree_kernel, n, m), out_shape=jax.ShapeD...]
    reduce_scatter x8 -> x0, waiting for transfers between devices: 153 us -> none  [the longest x4 108 us: shards(): lax.psum_scatter(partial_out.astype(jnp.bfloat16), 'tensor', scatter_dime...]
    all_gather x3 -> x0, waiting for transfers between devices: 78.8 us -> none  [shards(): gathered = lax.all_gather(fresh_share, 'tensor', axis=1, tiled=True)]
    dot_general x24 -> x0, matrix products: 36.4 us -> none  [the longest x4 16.4 us: shards(): jnp.dot(scaled, weights, preferred_element_type=jnp.float32)]
    psum x4 -> x0, blocking collectives: 26.6 us -> none  [shards(): total_sums = lax.psum(square_sums, 'dp')]
    all_gather x4 -> x0, blocking collectives: 21.7 us -> none  [shards(): lax.all_gather(attended, 'dp', axis=0, tiled=True)]
    gather x25 -> x0, local copies, waits for them, and re-layouts: 20.6 us -> none  [the longest x9 15.3 us: shards(): jnp.take_along_axis(previous, parents[:, tree_level - 1][:, :, None], axi...]
    reduce_sum x12 -> x0, other arithmetic: 9.44 us -> none  [the longest x4 7.89 us: shards(): square_sums = jnp.sum(flat_state * flat_state, axis=1)]
  transfers between devices with their start and end apart: 11 -> 0, of which waited for: 11 -> 0; matrix products, arithmetic and copies ran while one was open for 3% -> 0% of each run, Pallas kernels for 0% -> 0%
where the time goes in v1:
time: 195 us; the launch traced here: 194 us
  Pallas kernels  184 us (94%)
  local copies, waits for them, and re-layouts  5.85 us (3%)
  other arithmetic  4.26 us (2%)
    pallas_call x1, Pallas kernels, kernel_shards(): pl.pallas_call(functools.partial(tree_kernel, n, m), out_shape=jax.ShapeD...  184 us
    unnamed x2, local copies, waits for them, and re-layouts  5.5 us

profile of v1, /device:TPU:0, one launch (start us, length us, event | category | flops | bytes accessed | tf_op | source)
XLA Modules:
  0.0 194.4 jit_solution(16121865466816984462)
XLA Ops:
  0.0 0.8 add_bitcast_fusion
  0.8 0.1 copy.12
  0.9 0.1 eq.34
  1.0 0.1 iota_compare_fusion.1
  1.1 0.7 add_bitcast_fusion.1
  1.8 0.1 copy.11
  1.9 0.1 eq.30
  1.9 1.3 broadcast_in_dim.11
  3.2 0.6 pad_convert_fusion.own_hot_ref
  3.9 0.8 fusion.hot_ref
  4.6 3.2 %copy.15 = bf16[512,8,2,128]{3,1,2,0:T(8,128)(2,1)} copy(bf16[512,8,2,128]{3,2,1,0:T(2,128)(2,1)} %bitcast.10) | data formatting | bytes 4194304
  7.8 184.3 %shard_map.91 = bf16[16,4,8,1024]{3,2,1,0:T(8,128)(2,1)} custom-call(bf16[16,4096]{1,0:T(8,128)(2,1)} %root_ref.1, bf16[16,4,8,4096]{3,2,1,0:T(8,128)(2,1)} %emb_hbm.1, bf16[3,128,128]{2,1,0:T(8,128)(2,1)} %fusion.hot_ref, bf16[4,32,32]{2,1,0:T(8,128)(2,1)} %pad_convert_fusion.own_hot_ref, s32[4]{0:T(128)} %len_ref.1, bf16[4,2,512,128]{3,2,1,0:T(8,128)(2,1)} %cache_hbm.1, ...), custom_call_target="tpu_custom_call" | custom-call | tf_op jit(solution)/shard_map/pallas_call | solution.py:640
  192.1 2.3 %copy.17 = bf16[16,4,8,1024]{3,2,1,0:T(8,128)(2,1)} copy(bf16[16,4,8,1024]{3,2,1,0:T(8,128)(2,1)} %shard_map.91) | data formatting | bytes 2097152
  (2 shorter events, 0.0 us)

commit v2 on v1

--- a/solution.py
+++ b/solution.py
@@ -12,6 +12,7 @@
 BRANCH = 8
 DEPTHS = 4
 CACHE = 512
+BATCHES = 2
 
 
 epsilon = 1e-05
@@ -210,15 +211,24 @@
     t = lax.axis_index("tensor")
     d = lax.axis_index("dp")
     requests, feat = root_ref.shape
-    rows = requests * BRANCH
-    own = rows // m
     own_requests = requests // m
+    part_requests = own_requests // BATCHES
+    own = part_requests * BRANCH
+    rows = own * m
+    lanes = sums_send.shape[2]
     share = feat // n
     head_cols = wq.shape[1]
     heads = head_cols // HD
+    steps = BATCHES * DEPTHS
 
     def cols_of(s):
         return pl.ds(pl.multiple_of(s * share, share), share)
+
+    def batch_rows(b):
+        return [pl.ds(k * own_requests + b * part_requests, part_requests) for k in range(m)]
+
+    def joined(blocks, columns):
+        return jnp.concatenate(blocks, axis=0).astype(jnp.float32).reshape(rows, columns)
 
     loads = [
         pltpu.make_async_copy(emb_hbm.at[:, 0], emb0, load_sem.at[0]),
@@ -315,109 +325,195 @@
     def rs_wait(e, slot):
         rs_copy(e, 0, lax.rem(t + 1, n), slot).wait_recv()
 
-    row_id = lax.broadcasted_iota(jnp.int32, (rows, rows), 0)
-    col_id = lax.broadcasted_iota(jnp.int32, (rows, rows), 1)
-    eye = row_id == col_id
+    eye = lax.broadcasted_iota(jnp.int32, (rows, lanes), 0) == lax.broadcasted_iota(
+        jnp.int32, (rows, lanes), 1
+    )
 
     def to_lanes(column):
-        spread = jnp.where(eye, jnp.broadcast_to(column, (rows, rows)), 0.0)
-        return jnp.broadcast_to(jnp.sum(spread, axis=0, keepdims=True), (8, rows))
-
-    spread_id = lax.broadcasted_iota(jnp.int32, (rows, requests), 0) // BRANCH
-    root_hot = (
-        spread_id == lax.broadcasted_iota(jnp.int32, (rows, requests), 1)
-    ).astype(jnp.bfloat16)
+        spread = jnp.where(eye, jnp.broadcast_to(column, (rows, lanes)), 0.0)
+        return jnp.broadcast_to(jnp.sum(spread, axis=0, keepdims=True), (8, lanes))
+
+    def product(i, s, first=False):
+        block = scaled[i, s]
+        if first:
+            proj[:, :head_cols] = dot32(block, wq[cols_of(s)])
+            proj[:, head_cols:] = dot32(block, wkv[cols_of(s)])
+        else:
+            proj[:, :head_cols] += dot32(block, wq[cols_of(s)])
+            proj[:, head_cols:] += dot32(block, wkv[cols_of(s)])
+
+    def gather_wave(i, k):
+        before = t - k
+        after = t + k
+
+        @pl.when(before >= 0)
+        def _():
+            ag_copy(i, before, lax.rem(t + 1, n), before).wait_recv()
+
+            @pl.when(t < n - 1)
+            def _():
+                ag_copy(i, before, t + 1, before).start()
+
+        @pl.when(after < n)
+        def _():
+            ag_copy(i, after, lax.rem(t + 1, n), after).wait_recv()
+
+            @pl.when(t > 0)
+            def _():
+                ag_copy(i, after, t - 1, after).start()
+
+        @pl.when(before >= 0)
+        def _():
+            product(i, before)
+
+        @pl.when(after < n)
+        def _():
+            product(i, after)
+
+    def add_arrived(i, s):
+        rs_wait(i, s)
+        rs_send[i, s] = (part[s] + rs_recv[i, s].astype(jnp.float32)).astype(jnp.bfloat16)
+
+    def sum_wave(i, w):
+        right = n - 1 + t - w
+        left = w - (n - 1 - t)
+
+        @pl.when((t > 0) & (right <= n - 1) & (right > t))
+        def _():
+            add_arrived(i, right)
+            rs_right(i, right).start()
+
+        @pl.when((t < n - 1) & (left >= 0) & (left < t))
+        def _():
+            add_arrived(i, left)
+            rs_left(i, left).start()
+
+    def finish(i):
+        b = lax.rem(i, BATCHES)
+        e = i // BATCHES
+        total[...] = state[b] + part[t]
+
+        @pl.when(t > 0)
+        def _():
+            rs_wait(i, t)
+            total[...] += rs_recv[i, t].astype(jnp.float32)
+
+        @pl.when(t < n - 1)
+        def _():
+            rs_wait(i, n)
+            total[...] += rs_recv[i, n].astype(jnp.float32)
+
+        fresh = total[...]
+
+        @pl.when(e < DEPTHS - 1)
+        def _():
+            later = i + BATCHES
+            embeds = joined([emb_share[e, r] for r in batch_rows(b)], share)
+            node = dot32(hot_ref[i], fresh.astype(jnp.bfloat16)) + embeds
+            state[b] = node
+            scaled[later, t] = (node * gain_ref[:, cols_of(t)]).astype(jnp.bfloat16)
+
+            @pl.when(t < n - 1)
+            def _():
+                ag_copy(later, t, t + 1, t).start()
+
+            @pl.when(t > 0)
+            def _():
+                ag_copy(later, t, t - 1, n).start()
+
+            share_sums[later, n - 1] = to_lanes(jnp.sum(node * node, axis=1, keepdims=True))
+            for k in range(n - 1):
+                tsum_copy(later, k).start()
+
+        for k, r in enumerate(batch_rows(b)):
+            out_ref[r, pl.ds(e, 1)] = (
+                fresh[k * own : (k + 1) * own]
+                .reshape(part_requests, 1, BRANCH, share)
+                .astype(jnp.bfloat16)
+            )
+
+    row_id = lax.broadcasted_iota(jnp.int32, (rows, requests), 0)
+    request_id = lax.broadcasted_iota(jnp.int32, (rows, requests), 1)
     loads[0].wait()
-    squares = jnp.zeros((rows, 1), jnp.float32)
-    for s in range(n):
-        cols = slice(s * share, (s + 1) * share)
-        node = dot32(root_hot, root_ref[:, cols]) + emb0[:, :, cols].astype(jnp.float32).reshape(
-            rows, share
-        )
-        squares = squares + jnp.sum(node * node, axis=1, keepdims=True)
-        scaled[0, s] = (node * gain_ref[:, cols]).astype(jnp.bfloat16)
-
-        @pl.when(t == s)
-        def _():
-            state[...] = node
-
-    sums_send[0] = to_lanes(squares)
+
+    def first_states(b, carry):
+        place = row_id // BRANCH
+        request = (
+            place // part_requests * own_requests + b * part_requests + place % part_requests
+        )
+        root_hot = (request == request_id).astype(jnp.bfloat16)
+        squares = jnp.zeros((rows, 1), jnp.float32)
+        for s in range(n):
+            cols = slice(s * share, (s + 1) * share)
+            embeds = joined([emb0[r, :, cols] for r in batch_rows(b)], share)
+            node = dot32(root_hot, root_ref[:, cols]) + embeds
+            squares = squares + jnp.sum(node * node, axis=1, keepdims=True)
+            scaled[b, s] = (node * gain_ref[:, cols]).astype(jnp.bfloat16)
+
+            @pl.when(t == s)
+            def _():
+                state[b] = node
+
+        sums_send[b] = to_lanes(squares)
+        return carry
+
+    lax.fori_loop(0, BATCHES, first_states, 0)
     tree_keys[...] = jnp.zeros_like(tree_keys)
     tree_values[...] = jnp.zeros_like(tree_values)
     tree_mask[...] = jnp.zeros_like(tree_mask)
-    for load in loads[1:]:
-        load.wait()
-
-    def level(e, carry):
-        def product(s):
-            block = scaled[e, s]
-            proj[:, :head_cols] += dot32(block, wq[cols_of(s)])
-            proj[:, head_cols:] += dot32(block, wkv[cols_of(s)])
-
-        proj[...] = jnp.zeros_like(proj)
-        product(t)
-
-        for k in range(1, n):
-            before = t - k
-            after = t + k
-
-            @pl.when((before >= 0) & (e > 0))
-            def _():
-                ag_copy(e, before, lax.rem(t + 1, n), before).wait_recv()
-
-                @pl.when(t < n - 1)
-                def _():
-                    ag_copy(e, before, t + 1, before).start()
-
-            @pl.when((after < n) & (e > 0))
-            def _():
-                ag_copy(e, after, lax.rem(t + 1, n), after).wait_recv()
-
-                @pl.when(t > 0)
-                def _():
-                    ag_copy(e, after, t - 1, after).start()
-
-            @pl.when(before >= 0)
-            def _():
-                product(before)
-
-            @pl.when(after < n)
-            def _():
-                product(after)
+    loads[1].wait()
+    loads[2].wait()
+
+    def step(i, carry):
+        b = lax.rem(i, BATCHES)
+        e = i // BATCHES
+        later = i + BATCHES - 1
+        gathering = (i > 0) & (later < steps)
+
+        @pl.when(e == 0)
+        def _():
+            product(i, 0, True)
+            for s in range(1, n):
+                product(i, s)
 
         @pl.when(e > 0)
         def _():
-            summed = share_sums[e, n - 1]
+            gather_wave(i, n - 1)
+            summed = share_sums[i, n - 1]
             for k in range(n - 1):
-                tsum_copy(e, k).wait_recv()
-                summed = summed + share_sums[e, k]
-            sums_send[e] = summed
+                tsum_copy(i, k).wait_recv()
+                summed = summed + share_sums[i, k]
+            sums_send[i] = summed
 
         for k in range(m):
-            proj_send[e, k] = proj[k * own : (k + 1) * own].astype(jnp.bfloat16)
+            proj_send[i, k] = proj[k * own : (k + 1) * own].astype(jnp.bfloat16)
         for k in range(m - 1):
-            proj_copy(e, k).start()
-            dsum_copy(e, k).start()
+            proj_copy(i, k).start()
+            dsum_copy(i, k).start()
+
+        @pl.when(i > 0)
+        def _():
+            for w in range(2, n - 1):
+                sum_wave(i - 1, w)
 
         own_row = lax.broadcasted_iota(jnp.int32, (own, DEPTHS * own), 0)
         own_col = lax.broadcasted_iota(jnp.int32, (own, DEPTHS * own), 1)
         itself = (own_col == own_row + e * own).astype(jnp.float32)
-        above = dot32(own_hot_ref[e], tree_mask[...])
-        mask_now = itself + above
-        tree_mask[...] = mask_now.astype(jnp.bfloat16)
+        mask_now = itself + dot32(own_hot_ref[i], tree_mask[b])
+        tree_mask[b] = mask_now.astype(jnp.bfloat16)
 
         projected = proj[pl.ds(pl.multiple_of(d * own, own), own)]
-        summed = sums_send[e]
+        summed = sums_send[i]
         for k in range(m - 1):
-            proj_copy(e, k).wait_recv()
-            dsum_copy(e, k).wait_recv()
-            projected = projected + proj_recv[e, k].astype(jnp.float32)
-            summed = summed + sums_recv[e, k]
-        pick = lax.broadcasted_iota(jnp.int32, (own, rows), 1) == (
-            lax.broadcasted_iota(jnp.int32, (own, rows), 0) + d * own
+            proj_copy(i, k).wait_recv()
+            dsum_copy(i, k).wait_recv()
+            projected = projected + proj_recv[i, k].astype(jnp.float32)
+            summed = summed + sums_recv[i, k]
+        pick = lax.broadcasted_iota(jnp.int32, (own, lanes), 1) == (
+            lax.broadcasted_iota(jnp.int32, (own, lanes), 0) + d * own
         )
         own_sums = jnp.sum(
-            jnp.where(pick, jnp.broadcast_to(summed[0:1], (own, rows)), 0.0),
+            jnp.where(pick, jnp.broadcast_to(summed[0:1], (own, lanes)), 0.0),
             axis=1,
             keepdims=True,
         )
@@ -425,27 +521,32 @@
         projected = projected * inv_rms
         queries = jnp.concatenate(
             [
-                projected[:, h * HD : (h + 1) * HD].reshape(own_requests, 1, BRANCH, HD)
+                projected[:, h * HD : (h + 1) * HD].reshape(part_requests, 1, BRANCH, HD)
                 for h in range(heads)
             ],
             axis=1,
         ).reshape(own * heads, HD).astype(jnp.bfloat16)
         now = pl.ds(pl.multiple_of(e * own, own), own)
-        tree_keys[now] = projected[:, head_cols : head_cols + HD].astype(jnp.bfloat16)
-        tree_values[now] = projected[:, head_cols + HD :].astype(jnp.bfloat16)
+        tree_keys[b, now] = projected[:, head_cols : head_cols + HD].astype(jnp.bfloat16)
+        tree_values[b, now] = projected[:, head_cols + HD :].astype(jnp.bfloat16)
+
+        @pl.when(i == 0)
+        def _():
+            loads[3].wait()
 
         per = heads * BRANCH
-        tree_scores = dot32_t(queries, tree_keys[...]) * HD ** (-0.5)
+        tree_scores = dot32_t(queries, tree_keys[b]) * HD ** (-0.5)
         allowed = jnp.broadcast_to(
-            mask_now.reshape(own_requests, 1, BRANCH, DEPTHS * own),
-            (own_requests, heads, BRANCH, DEPTHS * own),
+            mask_now.reshape(part_requests, 1, BRANCH, DEPTHS * own),
+            (part_requests, heads, BRANCH, DEPTHS * own),
         ).reshape(own * heads, DEPTHS * own)
         tree_scores = jnp.where(allowed > 0.5, tree_scores, masked_score)
         cache_scores = []
         position = lax.broadcasted_iota(jnp.int32, (per, CACHE), 1)
-        for r in range(own_requests):
-            scores = dot32_t(queries[r * per : (r + 1) * per], cache[r, 0]) * HD ** (-0.5)
-            cache_scores.append(jnp.where(position < len_ref[r], scores, masked_score))
+        for r in range(part_requests):
+            request = b * part_requests + r
+            scores = dot32_t(queries[r * per : (r + 1) * per], cache[request, 0]) * HD ** (-0.5)
+            cache_scores.append(jnp.where(position < len_ref[request], scores, masked_score))
         cache_scores = jnp.concatenate(cache_scores, axis=0)
         row_max = jnp.maximum(
             jnp.max(cache_scores, axis=1, keepdims=True),
@@ -460,143 +561,109 @@
         tree_weights = (tree_exp / denominator).astype(jnp.bfloat16)
         mixed = jnp.concatenate(
             [
-                dot32(cache_weights[r * per : (r + 1) * per], cache[r, 1])
-                for r in range(own_requests)
+                dot32(cache_weights[r * per : (r + 1) * per], cache[b * part_requests + r, 1])
+                for r in range(part_requests)
             ],
             axis=0,
-        ) + dot32(tree_weights, tree_values[...])
-        mixed = mixed.reshape(own_requests, heads, BRANCH, HD)
+        ) + dot32(tree_weights, tree_values[b])
+        mixed = mixed.reshape(part_requests, heads, BRANCH, HD)
         for h in range(heads):
-            att[e, d, :, h * HD : (h + 1) * HD] = mixed[:, h].reshape(own, HD).astype(jnp.bfloat16)
+            att[i, d, :, h * HD : (h + 1) * HD] = mixed[:, h].reshape(own, HD).astype(jnp.bfloat16)
         for k in range(m - 1):
-            att_copy(e, k).start()
+            att_copy(i, k).start()
+
+        @pl.when(i > 0)
+        def _():
+            finish(i - 1)
+
+        @pl.when(gathering)
+        def _():
+            product(later, t, True)
+
         for k in range(m - 1):
-            att_copy(e, k).wait_recv()
-
-        attended = att[e].reshape(rows, head_cols)
-
-        def own_part(s):
-            part[s] = dot32(attended, wo[:, s * share : (s + 1) * share])
-
+            att_copy(i, k).wait_recv()
+
+        @pl.when(i == 0)
+        def _():
+            for load in loads[4:]:
+                load.wait()
+
+        attended = att[i].reshape(rows, head_cols)
         done = set()
-        for k in range(n - 1):
+        for k in range(n):
             right, left = n - 1 - k, k
             for s in (right, left):
                 if s not in done:
-                    own_part(s)
+                    part[s] = dot32(attended, wo[:, s * share : (s + 1) * share])
                     done.add(s)
-
-            @pl.when(t == 0)
-            def _():
-                rs_send[e, right] = part[right].astype(jnp.bfloat16)
-                rs_right(e, right).start()
-
-            @pl.when(t == n - 1)
-            def _():
-                rs_send[e, left] = part[left].astype(jnp.bfloat16)
-                rs_left(e, left).start()
-
-        def relay_right(s):
-            @pl.when((t > 0) & (t < s))
-            def _():
-                rs_wait(e, s)
-                rs_send[e, s] = (part[s] + rs_recv[e, s].astype(jnp.float32)).astype(jnp.bfloat16)
-                rs_right(e, s).start()
-
-        def relay_left(s):
-            @pl.when((t < n - 1) & (t > s))
-            def _():
-                rs_wait(e, s)
-                rs_send[e, s] = (part[s] + rs_recv[e, s].astype(jnp.float32)).astype(jnp.bfloat16)
-                rs_left(e, s).start()
-
-        @pl.when(t < n // 2)
+            if k < n - 1:
+
+                @pl.when(t == 0)
+                def _():
+                    rs_send[i, right] = part[right].astype(jnp.bfloat16)
+                    rs_right(i, right).start()
+
+                @pl.when(t == n - 1)
+                def _():
+                    rs_send[i, left] = part[left].astype(jnp.bfloat16)
+                    rs_left(i, left).start()
+
+        if n > 2:
+
+            @pl.when(gathering)
+            def _():
+                gather_wave(later, 1)
+
+            sum_wave(i, 1)
+
+            @pl.when(gathering)
+            def _():
+                for k in range(2, n - 1):
+                    gather_wave(later, k)
+
+        return carry
+
+    lax.fori_loop(0, steps, step, 0)
+    for w in range(2, n - 1):
+        sum_wave(steps - 1, w)
+    finish(steps - 1)
+
+    def drain(i, carry):
+        for k in range(m - 1):
+            proj_copy(i, k).wait_send()
+            dsum_copy(i, k).wait_send()
+            att_copy(i, k).wait_send()
+        for s in range(n):
+
+            @pl.when(t < s)
+            def _():
+                rs_right(i, s).wait_send()
+
+            @pl.when(t > s)
+            def _():
+                rs_left(i, s).wait_send()
+
+        @pl.when(i >= BATCHES)
         def _():
             for k in range(n - 1):
-                relay_right(n - 1 - k)
-                relay_left(k)
-
-        @pl.when(t >= n // 2)
-        def _():
-            for k in range(n - 1):
-                relay_left(k)
-                relay_right(n - 1 - k)
-
-        total[...] = state[...] + part[t]
-
-        @pl.when(t > 0)
-        def _():
-            rs_wait(e, t)
-            total[...] += rs_recv[e, t].astype(jnp.float32)
-
-        @pl.when(t < n - 1)
-        def _():
-            rs_wait(e, n)
-            total[...] += rs_recv[e, n].astype(jnp.float32)
-
-        fresh = total[...]
-        out_ref[:, pl.ds(e, 1)] = fresh.reshape(requests, 1, BRANCH, share).astype(jnp.bfloat16)
-
-        @pl.when(e < DEPTHS - 1)
-        def _():
-            node = dot32(hot_ref[e], fresh.astype(jnp.bfloat16)) + emb_share[e].astype(
-                jnp.float32
-            ).reshape(rows, share)
-            state[...] = node
-            scaled[e + 1, t] = (node * gain_ref[:, cols_of(t)]).astype(jnp.bfloat16)
-
-            @pl.when(t < n - 1)
-            def _():
-                ag_copy(e + 1, t, t + 1, t).start()
-
-            @pl.when(t > 0)
-            def _():
-                ag_copy(e + 1, t, t - 1, n).start()
-
-            share_sums[e + 1, n - 1] = to_lanes(jnp.sum(node * node, axis=1, keepdims=True))
-            for k in range(n - 1):
-                tsum_copy(e + 1, k).start()
-
-        return carry
-
-    lax.fori_loop(0, DEPTHS, level, 0)
-
-    def drain(e, carry):
-        for k in range(m - 1):
-            proj_copy(e, k).wait_send()
-            dsum_copy(e, k).wait_send()
-            att_copy(e, k).wait_send()
-        for s in range(n):
-
-            @pl.when(t < s)
-            def _():
-                rs_right(e, s).wait_send()
-
-            @pl.when(t > s)
-            def _():
-                rs_left(e, s).wait_send()
-
-        @pl.when(e > 0)
-        def _():
-            for k in range(n - 1):
-                tsum_copy(e, k).wait_send()
+                tsum_copy(i, k).wait_send()
             for s in range(n):
 
                 @pl.when((s <= t) & (t < n - 1))
                 def _():
-                    ag_copy(e, s, t + 1, s).wait_send()
+                    ag_copy(i, s, t + 1, s).wait_send()
 
                 @pl.when((s > t) & (t > 0))
                 def _():
-                    ag_copy(e, s, t - 1, s).wait_send()
+                    ag_copy(i, s, t - 1, s).wait_send()
 
             @pl.when(t > 0)
             def _():
-                ag_copy(e, t, t - 1, n).wait_send()
+                ag_copy(i, t, t - 1, n).wait_send()
 
         return carry
 
-    lax.fori_loop(0, DEPTHS, drain, 0)
+    lax.fori_loop(0, steps, drain, 0)
 
 
 def kernel_shards(
@@ -614,24 +681,29 @@
     m = lax.axis_size("dp")
     requests, feat = root_features.shape
     own_requests = cache_lengths.shape[0]
-    rows = requests * BRANCH
-    own = own_requests * BRANCH
+    part_requests = own_requests // BATCHES
+    own = part_requests * BRANCH
+    rows = own * m
+    lanes = -(-rows // 128) * 128
+    steps = BATCHES * DEPTHS
     share = feat // n
     head_cols = w_query.shape[1]
     proj_cols = head_cols + 2 * HD
 
     def one_hots(table):
-        count = table.shape[0]
-        first = (jnp.arange(count, dtype=jnp.int32) * BRANCH)[None, :, None]
-        index = (jnp.swapaxes(table, 0, 1) + first).reshape(DEPTHS - 1, count * BRANCH)
-        lane = jnp.arange(count * BRANCH, dtype=jnp.int32)
+        devices = table.shape[0] // own_requests
+        count = devices * own
+        split = table.reshape(devices, BATCHES, part_requests, DEPTHS - 1, BRANCH)
+        split = jnp.transpose(split, (3, 1, 0, 2, 4)).reshape((DEPTHS - 1) * BATCHES, count)
+        lane = jnp.arange(count, dtype=jnp.int32)
+        index = split + (lane // BRANCH * BRANCH)[None, :]
         return (index[:, :, None] == lane[None, None, :]).astype(jnp.bfloat16)
 
     hot = one_hots(parents)
     own_parents = lax.dynamic_slice_in_dim(
         parents, lax.axis_index("dp") * own_requests, own_requests, 0
     )
-    own_hot = jnp.pad(one_hots(own_parents), ((1, 0), (0, 0), (0, 0)))
+    own_hot = jnp.pad(one_hots(own_parents), ((BATCHES, 0), (0, 0), (0, 0)))
     bf16, f32 = jnp.bfloat16, jnp.float32
     vmem = pl.BlockSpec(memory_space=pltpu.VMEM)
     smem = pl.BlockSpec(memory_space=pltpu.SMEM)
@@ -649,35 +721,35 @@
             pltpu.VMEM((feat, head_cols), bf16),
             pltpu.VMEM((feat, 2 * HD), bf16),
             pltpu.VMEM((head_cols, feat), bf16),
-            pltpu.VMEM((DEPTHS, n, rows, share), bf16),
-            pltpu.VMEM((DEPTHS, n, 8, rows), f32),
-            pltpu.VMEM((rows, share), f32),
+            pltpu.VMEM((steps, n, rows, share), bf16),
+            pltpu.VMEM((steps, n, 8, lanes), f32),
+            pltpu.VMEM((BATCHES, rows, share), f32),
             pltpu.VMEM((rows, proj_cols), f32),
-            pltpu.VMEM((DEPTHS, m, own, proj_cols), bf16),
-            pltpu.VMEM((DEPTHS, m - 1, own, proj_cols), bf16),
-            pltpu.VMEM((DEPTHS, 8, rows), f32),
-            pltpu.VMEM((DEPTHS, m - 1, 8, rows), f32),
-            pltpu.VMEM((DEPTHS * own, HD), bf16),
-            pltpu.VMEM((DEPTHS * own, HD), bf16),
-            pltpu.VMEM((own, DEPTHS * own), bf16),
-            pltpu.VMEM((DEPTHS, m, own, head_cols), bf16),
+            pltpu.VMEM((steps, m, own, proj_cols), bf16),
+            pltpu.VMEM((steps, m - 1, own, proj_cols), bf16),
+            pltpu.VMEM((steps, 8, lanes), f32),
+            pltpu.VMEM((steps, m - 1, 8, lanes), f32),
+            pltpu.VMEM((BATCHES, DEPTHS * own, HD), bf16),
+            pltpu.VMEM((BATCHES, DEPTHS * own, HD), bf16),
+            pltpu.VMEM((BATCHES, own, DEPTHS * own), bf16),
+            pltpu.VMEM((steps, m, own, head_cols), bf16),
             pltpu.VMEM((n, rows, share), f32),
-            pltpu.VMEM((DEPTHS, n, rows, share), bf16),
-            pltpu.VMEM((DEPTHS, n + 1, rows, share), bf16),
+            pltpu.VMEM((steps, n, rows, share), bf16),
+            pltpu.VMEM((steps, n + 1, rows, share), bf16),
             pltpu.VMEM((rows, share), f32),
             dma((4 + DEPTHS,)),
-            dma((DEPTHS, n + 1)),
-            dma((DEPTHS, n)),
-            dma((DEPTHS, n - 1)),
-            dma((DEPTHS, n - 1)),
-            dma((DEPTHS, m - 1)),
-            dma((DEPTHS, m - 1)),
-            dma((DEPTHS, m - 1)),
-            dma((DEPTHS, m - 1)),
-            dma((DEPTHS, m - 1)),
-            dma((DEPTHS, m - 1)),
-            dma((DEPTHS, n)),
-            dma((DEPTHS, n + 1)),
+            dma((steps, n + 1)),
+            dma((steps, n)),
+            dma((steps, n - 1)),
+            dma((steps, n - 1)),
+            dma((steps, m - 1)),
+            dma((steps, m - 1)),
+            dma((steps, m - 1)),
+            dma((steps, m - 1)),
+            dma((steps, m - 1)),
+            dma((steps, m - 1)),
+            dma((steps, n)),
+            dma((steps, n + 1)),
         ],
         compiler_params=pltpu.CompilerParams(
             collective_id=0, has_side_effects=True, vmem_limit_bytes=60 * 1024 * 1024

time: 195 us -> 170 us (0.87)
  Pallas kernels: 184 us -> 159 us
    pallas_call x1, Pallas kernels: 184 us -> 159 us  [kernel_shards(): pl.pallas_call(functools.partial(tree_kernel, n, m), out_shape=jax.ShapeD...]
    unnamed x2 -> x3, local copies, waits for them, and re-layouts: 5.5 us -> 6.28 us
where the time goes in v2:
time: 170 us; the launch traced here: 169 us
  Pallas kernels  159 us (94%)
  local copies, waits for them, and re-layouts  7.34 us (4%)
  other arithmetic  2.79 us (2%)
    pallas_call x1, Pallas kernels, kernel_shards(): pl.pallas_call(functools.partial(tree_kernel, n, m), out_shape=jax.ShapeD...  159 us
    unnamed x3, local copies, waits for them, and re-layouts  6.28 us

profile of v2, /device:TPU:0, one launch (start us, length us, event | category | flops | bytes accessed | tf_op | source)
XLA Modules:
  0.0 169.2 jit_solution(10111193971053328644)
XLA Ops:
  0.0 0.8 constant_dynamic-slice_fusion
  0.8 0.1 copy.16
  0.9 0.1 reshape.80
  1.0 0.1 iota_compare_fusion.1
  1.1 1.3 broadcast_in_dim.6
  2.4 0.6 pad_convert_fusion.own_hot_ref
  3.0 0.8 copy.14
  3.8 0.1 reshape.78
  3.9 0.8 fusion.hot_ref
  4.6 3.2 %copy.19 = bf16[512,8,2,128]{3,1,2,0:T(8,128)(2,1)} copy(bf16[512,8,2,128]{3,2,1,0:T(2,128)(2,1)} %bitcast.14) | data formatting | bytes 4194304
  7.9 159.0 %shard_map.91 = bf16[16,4,8,1024]{3,2,1,0:T(8,128)(2,1)} custom-call(bf16[16,4096]{1,0:T(8,128)(2,1)} %root_ref.1, bf16[16,4,8,4096]{3,2,1,0:T(8,128)(2,1)} %emb_hbm.1, bf16[6,64,64]{2,1,0:T(8,128)(2,1)} %fusion.hot_ref, bf16[8,16,16]{2,1,0:T(8,128)(2,1)} %pad_convert_fusion.own_hot_ref, s32[4]{0:T(128)} %len_ref.1, bf16[4,2,512,128]{3,2,1,0:T(8,128)(2,1)} %cache_hbm.1, ...), custom_call_target="tpu_custom_call" | custom-call | tf_op jit(solution)/shard_map/pallas_call | solution.py:712
  166.9 2.3 %copy.21 = bf16[16,4,8,1024]{3,2,1,0:T(8,128)(2,1)} copy(bf16[16,4,8,1024]{3,2,1,0:T(8,128)(2,1)} %shard_map.91) | data formatting | bytes 2097152
  (5 shorter events, 0.0 us)

commit v3 on v2

--- a/solution.py
+++ b/solution.py
@@ -13,6 +13,7 @@
 DEPTHS = 4
 CACHE = 512
 BATCHES = 2
+SUBS = 2
 
 
 epsilon = 1e-05
@@ -164,7 +165,6 @@
     root_ref,
     emb_hbm,
     hot_ref,
-    own_hot_ref,
     len_ref,
     cache_hbm,
     gain_ref,
@@ -221,6 +221,11 @@
     heads = head_cols // HD
     steps = BATCHES * DEPTHS
 
+    sub = share // SUBS
+
+    def sub_of(s, u):
+        return pl.ds(pl.multiple_of(s * share + u * sub, sub), sub)
+
     def cols_of(s):
         return pl.ds(pl.multiple_of(s * share, share), share)
 
@@ -256,12 +261,12 @@
         pl.semaphore_signal(barrier, inc=1, device_id={"tensor": peer}, device_id_type=MESH)
     pl.semaphore_wait(barrier, m + n - 2)
 
-    def ag_copy(e, s, to, send_slot):
+    def ag_copy(e, s, u, to, send_slot):
         return pltpu.make_async_remote_copy(
-            src_ref=scaled.at[e, s],
-            dst_ref=scaled.at[e, s],
-            send_sem=ag_ssem.at[e, send_slot],
-            recv_sem=ag_rsem.at[e, s],
+            src_ref=scaled.at[e, s, u],
+            dst_ref=scaled.at[e, s, u],
+            send_sem=ag_ssem.at[e, send_slot, u],
+            recv_sem=ag_rsem.at[e, s, u],
             device_id={"tensor": to},
             device_id_type=MESH,
         )
@@ -306,24 +311,24 @@
             device_id_type=MESH,
         )
 
-    def rs_copy(e, s, to, slot):
+    def rs_copy(e, s, u, to, slot):
         return pltpu.make_async_remote_copy(
-            src_ref=rs_send.at[e, s],
-            dst_ref=rs_recv.at[e, slot],
-            send_sem=rs_ssem.at[e, s],
-            recv_sem=rs_rsem.at[e, slot],
+            src_ref=rs_send.at[e, s, u],
+            dst_ref=rs_recv.at[e, slot, u],
+            send_sem=rs_ssem.at[e, s, u],
+            recv_sem=rs_rsem.at[e, slot, u],
             device_id={"tensor": to},
             device_id_type=MESH,
         )
 
-    def rs_right(e, s):
-        return rs_copy(e, s, t + 1, s)
-
-    def rs_left(e, s):
-        return rs_copy(e, s, t - 1, jnp.where(t - 1 == s, n, s))
-
-    def rs_wait(e, slot):
-        rs_copy(e, 0, lax.rem(t + 1, n), slot).wait_recv()
+    def rs_right(e, s, u):
+        return rs_copy(e, s, u, t + 1, s)
+
+    def rs_left(e, s, u):
+        return rs_copy(e, s, u, t - 1, jnp.where(t - 1 == s, n, s))
+
+    def rs_wait(e, slot, u):
+        rs_copy(e, 0, u, lax.rem(t + 1, n), slot).wait_recv()
 
     eye = lax.broadcasted_iota(jnp.int32, (rows, lanes), 0) == lax.broadcasted_iota(
         jnp.int32, (rows, lanes), 1
@@ -334,103 +339,122 @@
         return jnp.broadcast_to(jnp.sum(spread, axis=0, keepdims=True), (8, lanes))
 
     def product(i, s, first=False):
-        block = scaled[i, s]
-        if first:
-            proj[:, :head_cols] = dot32(block, wq[cols_of(s)])
-            proj[:, head_cols:] = dot32(block, wkv[cols_of(s)])
-        else:
-            proj[:, :head_cols] += dot32(block, wq[cols_of(s)])
-            proj[:, head_cols:] += dot32(block, wkv[cols_of(s)])
+        for u in range(SUBS):
+            block = scaled[i, s, u]
+            cols = sub_of(s, u)
+            if first and u == 0:
+                proj[:, :head_cols] = dot32(block, wq[cols])
+                proj[:, head_cols:] = dot32(block, wkv[cols])
+            else:
+                proj[:, :head_cols] += dot32(block, wq[cols])
+                proj[:, head_cols:] += dot32(block, wkv[cols])
 
     def gather_wave(i, k):
         before = t - k
         after = t + k
 
+        for u in range(SUBS):
+
+            @pl.when(before >= 0)
+            def _():
+                ag_copy(i, before, u, lax.rem(t + 1, n), before).wait_recv()
+
+                @pl.when(t < n - 1)
+                def _():
+                    ag_copy(i, before, u, t + 1, before).start()
+
+            @pl.when(after < n)
+            def _():
+                ag_copy(i, after, u, lax.rem(t + 1, n), after).wait_recv()
+
+                @pl.when(t > 0)
+                def _():
+                    ag_copy(i, after, u, t - 1, after).start()
+
         @pl.when(before >= 0)
         def _():
-            ag_copy(i, before, lax.rem(t + 1, n), before).wait_recv()
-
-            @pl.when(t < n - 1)
-            def _():
-                ag_copy(i, before, t + 1, before).start()
+            product(i, before)
 
         @pl.when(after < n)
         def _():
-            ag_copy(i, after, lax.rem(t + 1, n), after).wait_recv()
-
-            @pl.when(t > 0)
-            def _():
-                ag_copy(i, after, t - 1, after).start()
-
-        @pl.when(before >= 0)
-        def _():
-            product(i, before)
-
-        @pl.when(after < n)
-        def _():
             product(i, after)
 
-    def add_arrived(i, s):
-        rs_wait(i, s)
-        rs_send[i, s] = (part[s] + rs_recv[i, s].astype(jnp.float32)).astype(jnp.bfloat16)
-
-    def sum_wave(i, w):
+    def add_arrived(i, s, u):
+        rs_wait(i, s, u)
+        rs_send[i, s, u] = (part[s, u] + rs_recv[i, s, u].astype(jnp.float32)).astype(
+            jnp.bfloat16
+        )
+
+    def sum_wave(i, w, u):
         right = n - 1 + t - w
         left = w - (n - 1 - t)
 
         @pl.when((t > 0) & (right <= n - 1) & (right > t))
         def _():
-            add_arrived(i, right)
-            rs_right(i, right).start()
+            add_arrived(i, right, u)
+            rs_right(i, right, u).start()
 
         @pl.when((t < n - 1) & (left >= 0) & (left < t))
         def _():
-            add_arrived(i, left)
-            rs_left(i, left).start()
+            add_arrived(i, left, u)
+            rs_left(i, left, u).start()
+
+    def later_waves(i):
+        for u in range(SUBS):
+            for w in range(1 if u else 2, n - 1):
+                sum_wave(i, w, u)
 
     def finish(i):
         b = lax.rem(i, BATCHES)
         e = i // BATCHES
-        total[...] = state[b] + part[t]
-
-        @pl.when(t > 0)
-        def _():
-            rs_wait(i, t)
-            total[...] += rs_recv[i, t].astype(jnp.float32)
-
-        @pl.when(t < n - 1)
-        def _():
-            rs_wait(i, n)
-            total[...] += rs_recv[i, n].astype(jnp.float32)
-
-        fresh = total[...]
-
-        @pl.when(e < DEPTHS - 1)
-        def _():
-            later = i + BATCHES
-            embeds = joined([emb_share[e, r] for r in batch_rows(b)], share)
-            node = dot32(hot_ref[i], fresh.astype(jnp.bfloat16)) + embeds
-            state[b] = node
-            scaled[later, t] = (node * gain_ref[:, cols_of(t)]).astype(jnp.bfloat16)
+        later = i + BATCHES
+        more = e < DEPTHS - 1
+        for u in range(SUBS):
+            cols = slice(u * sub, (u + 1) * sub)
+            total[u] = state[b, u] + part[t, u]
+
+            @pl.when(t > 0)
+            def _():
+                rs_wait(i, t, u)
+                total[u] += rs_recv[i, t, u].astype(jnp.float32)
 
             @pl.when(t < n - 1)
             def _():
-                ag_copy(later, t, t + 1, t).start()
-
-            @pl.when(t > 0)
+                rs_wait(i, n, u)
+                total[u] += rs_recv[i, n, u].astype(jnp.float32)
+
+            @pl.when(more)
             def _():
-                ag_copy(later, t, t - 1, n).start()
-
-            share_sums[later, n - 1] = to_lanes(jnp.sum(node * node, axis=1, keepdims=True))
+                embeds = joined([emb_share[e, r, :, cols] for r in batch_rows(b)], sub)
+                node = dot32(hot_ref[i], total[u].astype(jnp.bfloat16)) + embeds
+                state[b, u] = node
+                scaled[later, t, u] = (node * gain_ref[:, sub_of(t, u)].astype(jnp.float32)).astype(jnp.bfloat16)
+
+                @pl.when(t < n - 1)
+                def _():
+                    ag_copy(later, t, u, t + 1, t).start()
+
+                @pl.when(t > 0)
+                def _():
+                    ag_copy(later, t, u, t - 1, n).start()
+
+        @pl.when(more)
+        def _():
+            squares = jnp.zeros((rows, 1), jnp.float32)
+            for u in range(SUBS):
+                node = state[b, u]
+                squares = squares + jnp.sum(node * node, axis=1, keepdims=True)
+            share_sums[later, n - 1] = to_lanes(squares)
             for k in range(n - 1):
                 tsum_copy(later, k).start()
 
-        for k, r in enumerate(batch_rows(b)):
-            out_ref[r, pl.ds(e, 1)] = (
-                fresh[k * own : (k + 1) * own]
-                .reshape(part_requests, 1, BRANCH, share)
-                .astype(jnp.bfloat16)
-            )
+        for u in range(SUBS):
+            for k, r in enumerate(batch_rows(b)):
+                out_ref[r, pl.ds(e, 1), :, u * sub : (u + 1) * sub] = (
+                    total[u, k * own : (k + 1) * own]
+                    .reshape(part_requests, 1, BRANCH, sub)
+                    .astype(jnp.bfloat16)
+                )
 
     row_id = lax.broadcasted_iota(jnp.int32, (rows, requests), 0)
     request_id = lax.broadcasted_iota(jnp.int32, (rows, requests), 1)
@@ -448,11 +472,14 @@
             embeds = joined([emb0[r, :, cols] for r in batch_rows(b)], share)
             node = dot32(root_hot, root_ref[:, cols]) + embeds
             squares = squares + jnp.sum(node * node, axis=1, keepdims=True)
-            scaled[b, s] = (node * gain_ref[:, cols]).astype(jnp.bfloat16)
+            fed = (node * gain_ref[:, cols].astype(jnp.float32)).astype(jnp.bfloat16)
+            for u in range(SUBS):
+                scaled[b, s, u] = fed[:, u * sub : (u + 1) * sub]
 
             @pl.when(t == s)
             def _():
-                state[b] = node
+                for u in range(SUBS):
+                    state[b, u] = node[:, u * sub : (u + 1) * sub]
 
         sums_send[b] = to_lanes(squares)
         return carry
@@ -493,14 +520,14 @@
 
         @pl.when(i > 0)
         def _():
-            for w in range(2, n - 1):
-                sum_wave(i - 1, w)
+            later_waves(i - 1)
 
         own_row = lax.broadcasted_iota(jnp.int32, (own, DEPTHS * own), 0)
         own_col = lax.broadcasted_iota(jnp.int32, (own, DEPTHS * own), 1)
         itself = (own_col == own_row + e * own).astype(jnp.float32)
-        mask_now = itself + dot32(own_hot_ref[i], tree_mask[b])
-        tree_mask[b] = mask_now.astype(jnp.bfloat16)
+        own_rows = pl.ds(pl.multiple_of(d * own, own), own)
+        mask_now = itself + dot32(hot_ref[jnp.maximum(i - BATCHES, 0), own_rows], tree_mask[b])
+        tree_mask[b, own_rows] = mask_now.astype(jnp.bfloat16)
 
         projected = proj[pl.ds(pl.multiple_of(d * own, own), own)]
         summed = sums_send[i]
@@ -589,24 +616,26 @@
                 load.wait()
 
         attended = att[i].reshape(rows, head_cols)
-        done = set()
-        for k in range(n):
-            right, left = n - 1 - k, k
-            for s in (right, left):
-                if s not in done:
-                    part[s] = dot32(attended, wo[:, s * share : (s + 1) * share])
-                    done.add(s)
-            if k < n - 1:
-
-                @pl.when(t == 0)
-                def _():
-                    rs_send[i, right] = part[right].astype(jnp.bfloat16)
-                    rs_right(i, right).start()
-
-                @pl.when(t == n - 1)
-                def _():
-                    rs_send[i, left] = part[left].astype(jnp.bfloat16)
-                    rs_left(i, left).start()
+        for u in range(SUBS):
+            done = set()
+            for k in range(n):
+                right, left = n - 1 - k, k
+                for s in (right, left):
+                    if s not in done:
+                        low = s * share + u * sub
+                        part[s, u] = dot32(attended, wo[:, low : low + sub])
+                        done.add(s)
+                if k < n - 1:
+
+                    @pl.when(t == 0)
+                    def _():
+                        rs_send[i, right, u] = part[right, u].astype(jnp.bfloat16)
+                        rs_right(i, right, u).start()
+
+                    @pl.when(t == n - 1)
+                    def _():
+                        rs_send[i, left, u] = part[left, u].astype(jnp.bfloat16)
+                        rs_left(i, left, u).start()
 
         if n > 2:
 
@@ -614,7 +643,7 @@
             def _():
                 gather_wave(later, 1)
 
-            sum_wave(i, 1)
+            sum_wave(i, 1, 0)
 
             @pl.when(gathering)
             def _():
@@ -624,8 +653,7 @@
         return carry
 
     lax.fori_loop(0, steps, step, 0)
-    for w in range(2, n - 1):
-        sum_wave(steps - 1, w)
+    later_waves(steps - 1)
     finish(steps - 1)
 
     def drain(i, carry):
@@ -633,33 +661,35 @@
             proj_copy(i, k).wait_send()
             dsum_copy(i, k).wait_send()
             att_copy(i, k).wait_send()
-        for s in range(n):
-
-            @pl.when(t < s)
-            def _():
-                rs_right(i, s).wait_send()
-
-            @pl.when(t > s)
-            def _():
-                rs_left(i, s).wait_send()
+        for u in range(SUBS):
+            for s in range(n):
+
+                @pl.when(t < s)
+                def _():
+                    rs_right(i, s, u).wait_send()
+
+                @pl.when(t > s)
+                def _():
+                    rs_left(i, s, u).wait_send()
 
         @pl.when(i >= BATCHES)
         def _():
             for k in range(n - 1):
                 tsum_copy(i, k).wait_send()
-            for s in range(n):
-
-                @pl.when((s <= t) & (t < n - 1))
+            for u in range(SUBS):
+                for s in range(n):
+
+                    @pl.when((s <= t) & (t < n - 1))
+                    def _():
+                        ag_copy(i, s, u, t + 1, s).wait_send()
+
+                    @pl.when((s > t) & (t > 0))
+                    def _():
+                        ag_copy(i, s, u, t - 1, s).wait_send()
+
+                @pl.when(t > 0)
                 def _():
-                    ag_copy(i, s, t + 1, s).wait_send()
-
-                @pl.when((s > t) & (t > 0))
-                def _():
-                    ag_copy(i, s, t - 1, s).wait_send()
-
-            @pl.when(t > 0)
-            def _():
-                ag_copy(i, t, t - 1, n).wait_send()
+                    ag_copy(i, t, u, t - 1, n).wait_send()
 
         return carry
 
@@ -691,19 +721,14 @@
     proj_cols = head_cols + 2 * HD
 
     def one_hots(table):
-        devices = table.shape[0] // own_requests
-        count = devices * own
-        split = table.reshape(devices, BATCHES, part_requests, DEPTHS - 1, BRANCH)
+        count = rows
+        split = table.reshape(m, BATCHES, part_requests, DEPTHS - 1, BRANCH)
         split = jnp.transpose(split, (3, 1, 0, 2, 4)).reshape((DEPTHS - 1) * BATCHES, count)
         lane = jnp.arange(count, dtype=jnp.int32)
         index = split + (lane // BRANCH * BRANCH)[None, :]
         return (index[:, :, None] == lane[None, None, :]).astype(jnp.bfloat16)
 
     hot = one_hots(parents)
-    own_parents = lax.dynamic_slice_in_dim(
-        parents, lax.axis_index("dp") * own_requests, own_requests, 0
-    )
-    own_hot = jnp.pad(one_hots(own_parents), ((BATCHES, 0), (0, 0), (0, 0)))
     bf16, f32 = jnp.bfloat16, jnp.float32
     vmem = pl.BlockSpec(memory_space=pltpu.VMEM)
     smem = pl.BlockSpec(memory_space=pltpu.SMEM)
@@ -712,7 +737,7 @@
     return pl.pallas_call(
         functools.partial(tree_kernel, n, m),
         out_shape=jax.ShapeDtypeStruct((requests, DEPTHS, BRANCH, share), bf16),
-        in_specs=[vmem, hbm, vmem, vmem, smem, hbm, vmem, hbm, hbm, hbm],
+        in_specs=[vmem, hbm, vmem, smem, hbm, vmem, hbm, hbm, hbm],
         out_specs=vmem,
         scratch_shapes=[
             pltpu.VMEM((requests, BRANCH, feat), bf16),
@@ -721,9 +746,9 @@
             pltpu.VMEM((feat, head_cols), bf16),
             pltpu.VMEM((feat, 2 * HD), bf16),
             pltpu.VMEM((head_cols, feat), bf16),
-            pltpu.VMEM((steps, n, rows, share), bf16),
+            pltpu.VMEM((steps, n, SUBS, rows, share // SUBS), bf16),
             pltpu.VMEM((steps, n, 8, lanes), f32),
-            pltpu.VMEM((BATCHES, rows, share), f32),
+            pltpu.VMEM((BATCHES, SUBS, rows, share // SUBS), f32),
             pltpu.VMEM((rows, proj_cols), f32),
             pltpu.VMEM((steps, m, own, proj_cols), bf16),
             pltpu.VMEM((steps, m - 1, own, proj_cols), bf16),
@@ -731,15 +756,15 @@
             pltpu.VMEM((steps, m - 1, 8, lanes), f32),
             pltpu.VMEM((BATCHES, DEPTHS * own, HD), bf16),
             pltpu.VMEM((BATCHES, DEPTHS * own, HD), bf16),
-            pltpu.VMEM((BATCHES, own, DEPTHS * own), bf16),
+            pltpu.VMEM((BATCHES, rows, DEPTHS * own), bf16),
             pltpu.VMEM((steps, m, own, head_cols), bf16),
-            pltpu.VMEM((n, rows, share), f32),
-            pltpu.VMEM((steps, n, rows, share), bf16),
-            pltpu.VMEM((steps, n + 1, rows, share), bf16),
-            pltpu.VMEM((rows, share), f32),
+            pltpu.VMEM((n, SUBS, rows, share // SUBS), f32),
+            pltpu.VMEM((steps, n, SUBS, rows, share // SUBS), bf16),
+            pltpu.VMEM((steps, n + 1, SUBS, rows, share // SUBS), bf16),
+            pltpu.VMEM((SUBS, rows, share // SUBS), f32),
             dma((4 + DEPTHS,)),
-            dma((steps, n + 1)),
-            dma((steps, n)),
+            dma((steps, n + 1, SUBS)),
+            dma((steps, n, SUBS)),
             dma((steps, n - 1)),
             dma((steps, n - 1)),
             dma((steps, m - 1)),
@@ -748,8 +773,8 @@
             dma((steps, m - 1)),
             dma((steps, m - 1)),
             dma((steps, m - 1)),
-            dma((steps, n)),
-            dma((steps, n + 1)),
+            dma((steps, n, SUBS)),
+            dma((steps, n + 1, SUBS)),
         ],
         compiler_params=pltpu.CompilerParams(
             collective_id=0, has_side_effects=True, vmem_limit_bytes=60 * 1024 * 1024
@@ -758,10 +783,9 @@
         root_features,
         branch_embeds,
         hot,
-        own_hot,
         cache_lengths,
         cache_kv,
-        norm_gain.astype(f32)[None, :],
+        norm_gain[None, :],
         w_query,
         w_keyval.reshape(feat, 2 * HD),
         w_out,

time: 170 us -> 163 us (0.959)
  Pallas kernels: 159 us -> 155 us
  other arithmetic: 2.79 us -> 0.78 us
    pallas_call x1, Pallas kernels: 159 us -> 155 us  [kernel_shards(): pl.pallas_call(functools.partial(tree_kernel, n, m), out_shape=jax.ShapeD...]
where the time goes in v3:
time: 163 us
  Pallas kernels  155 us (95%)
  local copies, waits for them, and re-layouts  7.69 us (5%)
    pallas_call x1, Pallas kernels, kernel_shards(): pl.pallas_call(functools.partial(tree_kernel, n, m), out_shape=jax.ShapeD...  155 us
    unnamed x3, local copies, waits for them, and re-layouts  6.28 us

profile of v3, /device:TPU:0, one launch (start us, length us, event | category | flops | bytes accessed | tf_op | source)
XLA Modules:
  0.0 163.1 jit_solution(16117799610304709596)
XLA Ops:
  0.0 1.3 broadcast_in_dim.2.gain_ref
  1.3 0.8 copy.12
  2.1 0.1 reshape.41
  2.2 0.8 fusion.hot_ref
  3.0 3.2 %copy.16 = bf16[512,8,2,128]{3,1,2,0:T(8,128)(2,1)} copy(bf16[512,8,2,128]{3,2,1,0:T(2,128)(2,1)} %bitcast.8) | data formatting | bytes 4194304
  6.2 154.6 %shard_map.91 = bf16[16,4,8,1024]{3,2,1,0:T(8,128)(2,1)} custom-call(bf16[16,4096]{1,0:T(8,128)(2,1)} %root_ref.1, bf16[16,4,8,4096]{3,2,1,0:T(8,128)(2,1)} %emb_hbm.1, bf16[6,64,64]{2,1,0:T(8,128)(2,1)} %fusion.hot_ref, s32[4]{0:T(128)} %len_ref.1, bf16[4,2,512,128]{3,2,1,0:T(8,128)(2,1)} %cache_hbm.1, bf16[1,4096]{1,0:T(2,128)(2,1)} %broadcast_in_dim.2.gain_ref, ...), custom_call_target="tpu_custom_call" | custom-call | tf_op jit(solution)/shard_map/pallas_call | solution.py:737
  160.8 2.3 %copy.18 = bf16[16,4,8,1024]{3,2,1,0:T(8,128)(2,1)} copy(bf16[16,4,8,1024]{3,2,1,0:T(8,128)(2,1)} %shard_map.91) | data formatting | bytes 2097152
  (3 shorter events, 0.0 us)
